TPU v7x, 256 devices: a whole 4x4x8 slice. The times are simulated.
256 devices in a mesh: region: 16 (over y, z_hi), dev: 16 (over x, z_lo, core).
Axes of the slice: x: 4, y: 4, z: 8 (z_hi: 4, z_lo: 2; z = z_hi * 2 + z_lo), core: 2. Of those that a mesh axis runs over, the one named last changes fastest.
Arguments:
- interior: float32 [16, 16, 384, 384], P('region', 'dev'), may hold values from -6.5 to 8.5, as said below
- coupling: float32 [16, 16, 384, 640], P('region', 'dev'), may hold values from -1 to 1
- tile_mask: int32 [16, 16, 5], P('region', 'dev'), may hold values 0 or 1
- prior: float32 [16, 640, 640], P('region', 'dev'), may hold values from -3.5 to 6, as said below
- sep_map: int32 [16, 384], P('region'), may hold values from 0 to 383, each once within a row
- nat_diag: float32 [384], replicated, may hold values from 0.25 to 2.5
Outputs:
- interior_cov: float32 [16, 16, 384, 384], P('region', 'dev')
- regional_cov: float32 [16, 640, 640], P('region', 'dev')
Inputs may be any that keep to these rules, and one draw needn't show every extreme that they name: `interior`: symmetric positive definite, smallest eigenvalue 0.5 or more. `prior`: symmetric positive definite. `sep_map`: each region's row names every national separator once.
All inputs are finite; a program needn't handle non-finite values. No bound on the sum of `tile_mask` on one device may be relied on, other than what follows from the above.
Results may differ from a plain program's by a relative error of at most 0.00011.
Values sent between devices are 32-bit elements; how exact they have to be, the bound alone decides.
A program may use at most 64 MiB of HBM per device.

v0:
```python
import jax
import jax.numpy as jnp
from jax import lax
from jax.sharding import PartitionSpec as P

NI = 384
ELIMINATED_COUNT = 256
NS = 384
TILE = 128
NRC = 640


FULL_PRECISION = lax.Precision.HIGHEST


def lower_solve(chol, right):
    return lax.linalg.triangular_solve(chol, right, left_side=True, lower=True, transpose_a=False)


def upper_solve(chol, right):
    return lax.linalg.triangular_solve(chol, right, left_side=True, lower=True, transpose_a=True)


def chol_apply(chol, right):
    return upper_solve(chol, lower_solve(chol, right))


def body(interior, coupling, tile_mask, prior, sep_map, nat_diag):
    dev_count = lax.axis_size("dev")
    own = lax.axis_index("dev")
    rows = NRC // dev_count
    scale = jnp.repeat(tile_mask[0, 0].astype(jnp.float32), TILE)
    masked = coupling[0, 0] * scale[None, :]
    chol = jnp.linalg.cholesky(interior[0, 0])
    solved = lower_solve(chol, masked)
    term = lax.dot_general(
        solved,
        solved,
        (((0,), (0,)), ((), ())),
        precision=FULL_PRECISION,
        preferred_element_type=jnp.float32,
    )
    placed = jnp.zeros((NRC, NRC), jnp.float32)
    placed = lax.dynamic_update_slice(placed, prior[0], (own * rows, jnp.int32(0)))
    complement_matrix = lax.psum(placed - term, "dev")
    eliminated_rows = complement_matrix[:ELIMINATED_COUNT, :ELIMINATED_COUNT]
    cross = complement_matrix[:ELIMINATED_COUNT, ELIMINATED_COUNT:]
    sep_block = complement_matrix[ELIMINATED_COUNT:, ELIMINATED_COUNT:]
    eliminated_factor = jnp.linalg.cholesky(eliminated_rows)
    weight_matrix = chol_apply(eliminated_factor, cross)
    local = sep_map[0]
    inverse = jnp.zeros((NS,), jnp.int32).at[local].set(jnp.arange(NS, dtype=jnp.int32))
    reduced = sep_block - lax.dot_general(
        cross,
        weight_matrix,
        (((0,), (0,)), ((), ())),
        precision=FULL_PRECISION,
        preferred_element_type=jnp.float32,
    )
    national_part = jnp.take(jnp.take(reduced, inverse, axis=0), inverse, axis=1)
    total = lax.psum(national_part, "region")
    normal_mat = total + jnp.diag(nat_diag)
    chol_n = jnp.linalg.cholesky(normal_mat)
    cov_nat = chol_apply(chol_n, jnp.eye(NS, dtype=jnp.float32))
    cov_sep = jnp.take(jnp.take(cov_nat, local, axis=0), local, axis=1)
    cross_covariance = -jnp.dot(
        weight_matrix, cov_sep, precision=FULL_PRECISION, preferred_element_type=jnp.float32
    )
    inverse_eliminated_block = chol_apply(
        eliminated_factor, jnp.eye(ELIMINATED_COUNT, dtype=jnp.float32)
    )
    eliminated_covariance = inverse_eliminated_block - lax.dot_general(
        cross_covariance,
        weight_matrix,
        (((1,), (1,)), ((), ())),
        precision=FULL_PRECISION,
        preferred_element_type=jnp.float32,
    )
    upper_rows = jnp.concatenate([eliminated_covariance, cross_covariance], axis=1)
    bottom = jnp.concatenate([cross_covariance.T, cov_sep], axis=1)
    cov_full = jnp.concatenate([upper_rows, bottom], axis=0)
    own_rows = lax.dynamic_slice_in_dim(cov_full, own * rows, rows, 0)
    middle = jnp.dot(solved, cov_full, precision=FULL_PRECISION, preferred_element_type=jnp.float32)
    inner = jnp.eye(NI, dtype=jnp.float32) + lax.dot_general(
        middle,
        solved,
        (((1,), (1,)), ((), ())),
        precision=FULL_PRECISION,
        preferred_element_type=jnp.float32,
    )
    left = upper_solve(chol, inner)
    result = upper_solve(chol, left.T)
    return (result[None, None], own_rows[None])


def solution(mesh):
    placed = (
        P("region", "dev", None, None),
        P("region", "dev", None, None),
        P("region", "dev", None),
        P("region", "dev", None),
        P("region", None),
        P(),
    )
    return jax.shard_map(
        body,
        mesh=mesh,
        in_specs=placed,
        out_specs=(P("region", "dev", None, None), P("region", "dev", None)),
        check_vma=False,
    )
```

profile of v0, /device:TPU:2, one launch (start us, length us, event | category | flops | bytes accessed | tf_op | source)
XLA Modules:
  0.0 626.6 jit_solution(9199766929516099718)
XLA Ops:
  7.2 1.3 copy.35
  8.5 1.1 fusion.5
  9.7 11.7 %cholesky.287 = f32[128,128]{1,0:T(8,128)S(1)} custom-call(f32[128,128]{1,0:T(8,128)S(1)} %cholesky.381), custom_call_target="Cholesky" | custom-call | tf_op jit(solution)/shard_map/jit(cholesky)/cholesky | solution.py:34
  21.4 9.8 %custom-call.47 = f32[1,128,128]{1,2,0:T(8,128)S(1)} custom-call(f32[1,128,128]{2,1,0:T(8,128)S(1)} %get-tuple-element.135), custom_call_target="InvertDiagBlocksLowerTriangular" | custom-call | tf_op jit(solution)/shard_map/jit(cholesky)/cholesky | solution.py:34
  32.0 11.7 %cholesky.306 = f32[128,128]{1,0:T(8,128)S(1)} custom-call(f32[128,128]{1,0:T(8,128)S(1)} %cholesky.385), custom_call_target="Cholesky" | custom-call | tf_op jit(solution)/shard_map/jit(cholesky)/cholesky | solution.py:34
  43.8 10.1 %custom-call.48 = f32[1,128,128]{1,2,0:T(8,128)S(1)} custom-call(f32[1,128,128]{2,1,0:T(8,128)S(1)} %get-tuple-element.133), custom_call_target="InvertDiagBlocksLowerTriangular" | custom-call | tf_op jit(solution)/shard_map/jit(cholesky)/cholesky/custom-call.6 | solution.py:34
  54.7 11.7 %cholesky.321 = f32[128,128]{1,0:T(8,128)S(1)} custom-call(f32[128,128]{1,0:T(8,128)S(1)} %convolution_subtract_fusion.21), custom_call_target="Cholesky" | custom-call | tf_op jit(solution)/shard_map/jit(cholesky)/cholesky | solution.py:34
  66.6 0.7 compare_reduce_fusion.3
  70.0 6.4 %while.11 = (s32[]{:T(128)}, f32[384,384]{0,1:T(8,128)S(1)}, s32[3,2]{0,1:T(2,128)S(1)}, f32[3,128,128]{2,1,0:T(8,128)S(1)}, s32[]{:T(128)}) while((s32[]{:T(128)}, f32[384,384]{0,1:T(8,128)S(1)}, s32[3,2]{0,1:T(2,128)S(1)}, f32[3,128,128]{2,1,0:T(8,128)S(1)}, s32[]{:T(128)}) %tuple.84), condition=%wide.while_cond.clone.1, body=%wide.while_body.clone.1.sunk | while | flops 2 | bytes 393321 | solution.py:21
  70.7 1.3 dynamic-slice.31
  72.8 1.3 dynamic-slice.31
  75.0 1.3 dynamic-slice.31
  76.4 29.5 %custom-call.54 = f32[3,128,128]{1,2,0:T(8,128)S(1)} custom-call(f32[3,128,128]{2,1,0:T(8,128)S(1)} %get-tuple-element.53), custom_call_target="InvertDiagBlocksLowerTriangular" | custom-call | tf_op jit(solution)/shard_map/triangular_solve/custom-call.13 | solution.py:21
  108.9 4.7 dynamic_update_slice.3
  113.6 4.2 convolution_subtract_fusion
  118.6 3.1 scatter_custom_fusion
  121.7 0.7 iota_compare_fusion.1
  122.4 0.9 fusion.23
  123.3 120.0 %all-reduce.5.cloned.1.call-done = f32[640,640]{0,1:T(8,128)} async-done(((f32[640,640]{0,1:T(8,128)}), f32[640,640]{0,1:T(8,128)}) %all-reduce.5.cloned.1.call-update) | async-done | bytes 1638416 | tf_op jit(solution)/shard_map/psum | solution.py:45
  243.4 1.0 slice.267
  244.5 1.0 fusion.24
  245.5 11.7 %cholesky.164 = f32[128,128]{1,0:T(8,128)S(1)} custom-call(f32[128,128]{1,0:T(8,128)S(1)} %cholesky.389), custom_call_target="Cholesky" | custom-call | tf_op jit(solution)/shard_map/jit(cholesky)/cholesky | solution.py:49
  257.3 9.8 %custom-call.49 = f32[1,128,128]{1,2,0:T(8,128)S(1)} custom-call(f32[1,128,128]{2,1,0:T(8,128)S(1)} %get-tuple-element.131), custom_call_target="InvertDiagBlocksLowerTriangular" | custom-call | tf_op jit(solution)/shard_map/jit(cholesky)/cholesky/custom-call.6 | solution.py:49
  267.6 11.7 %cholesky.178 = f32[128,128]{1,0:T(8,128)S(1)} custom-call(f32[128,128]{1,0:T(8,128)S(1)} %convolution_subtract_fusion.20), custom_call_target="Cholesky" | custom-call | tf_op jit(solution)/shard_map/jit(cholesky)/cholesky | solution.py:49
  281.9 4.0 while.9
  282.7 1.3 bitcast_dynamic-update-slice_fusion.6
  284.6 1.3 bitcast_dynamic-update-slice_fusion.6
  285.9 19.7 %custom-call.38 = f32[2,128,128]{1,2,0:T(8,128)S(1)} custom-call(f32[2,128,128]{2,1,0:T(8,128)S(1)} %get-tuple-element.30), custom_call_target="InvertDiagBlocksLowerTriangular" | custom-call | tf_op jit(solution)/shard_map/triangular_solve | solution.py:21
  306.1 1.0 fusion.81
  307.0 1.3 fusion.29
  308.4 1.4 convolution_subtract_fusion.14
  311.2 2.0 convolution_subtract_fusion.1
  313.5 1.7 gather_fusion
  315.2 0.9 broadcast_select_fusion.1
  316.2 1.3 copy.50
  317.5 2.1 gather_fusion.1
  319.6 0.9 select_bitcast_fusion.1
  321.2 0.9 fusion.77
  322.1 172.6 %all-reduce.7.cloned.1.call-done = f32[384,384]{0,1:T(8,128)} async-done(((f32[384,384]{0,1:T(8,128)}), f32[384,384]{0,1:T(8,128)}) %all-reduce.7.cloned.1.call-update) | async-done | bytes 589840 | tf_op jit(solution)/shard_map/psum | solution.py:61
  494.7 1.2 select_add_fusion
  496.3 11.7 %cholesky.336 = f32[128,128]{1,0:T(8,128)S(1)} custom-call(f32[128,128]{1,0:T(8,128)S(1)} %cholesky.392), custom_call_target="Cholesky" | custom-call | tf_op jit(solution)/shard_map/jit(cholesky)/cholesky | solution.py:63
  508.0 9.8 %custom-call.50 = f32[1,128,128]{1,2,0:T(8,128)S(1)} custom-call(f32[1,128,128]{2,1,0:T(8,128)S(1)} %get-tuple-element.127), custom_call_target="InvertDiagBlocksLowerTriangular" | custom-call | tf_op jit(solution)/shard_map/jit(cholesky)/cholesky | solution.py:63
  518.4 11.7 %cholesky.355 = f32[128,128]{1,0:T(8,128)S(1)} custom-call(f32[128,128]{1,0:T(8,128)S(1)} %cholesky.396), custom_call_target="Cholesky" | custom-call | tf_op jit(solution)/shard_map/jit(cholesky)/cholesky | solution.py:63
  531.0 9.9 %custom-call.51 = f32[1,128,128]{1,2,0:T(8,128)S(1)} custom-call(f32[1,128,128]{2,1,0:T(8,128)S(1)} %get-tuple-element.125), custom_call_target="InvertDiagBlocksLowerTriangular" | custom-call | tf_op jit(solution)/shard_map/jit(cholesky)/cholesky/custom-call.6 | solution.py:63
  541.7 11.7 %cholesky.370 = f32[128,128]{1,0:T(8,128)S(1)} custom-call(f32[128,128]{1,0:T(8,128)S(1)} %convolution_subtract_fusion.19), custom_call_target="Cholesky" | custom-call | tf_op jit(solution)/shard_map/jit(cholesky)/cholesky | solution.py:63
  554.8 0.7 compare_reduce_fusion
  557.6 6.3 %while.10 = (s32[]{:T(128)}, f32[384,384]{0,1:T(8,128)S(1)}, s32[3,2]{0,1:T(2,128)S(1)}, f32[3,128,128]{2,1,0:T(8,128)S(1)}, s32[]{:T(128)}) while((s32[]{:T(128)}, f32[384,384]{0,1:T(8,128)S(1)}, s32[3,2]{0,1:T(2,128)S(1)}, f32[3,128,128]{2,1,0:T(8,128)S(1)}, s32[]{:T(128)}) %tuple.97), condition=%wide.while_cond, body=%wide.while_body.sunk | while | flops 2 | bytes 393321 | solution.py:21
  558.2 1.4 dynamic-slice.29
  560.3 1.4 dynamic-slice.29
  562.4 1.4 dynamic-slice.29
  564.0 29.5 %custom-call.52 = f32[3,128,128]{1,2,0:T(8,128)S(1)} custom-call(f32[3,128,128]{2,1,0:T(8,128)S(1)} %get-tuple-element.51), custom_call_target="InvertDiagBlocksLowerTriangular" | custom-call | tf_op jit(solution)/shard_map/triangular_solve/custom-call.13 | solution.py:21
  593.5 1.1 fusion.31
  595.4 0.8 convolution_subtract_fusion.11
  598.4 1.9 gather_fusion.2
  600.7 1.7 gather_fusion.3
  602.6 0.9 convolution_negate_fusion
  604.2 1.1 copy.60
  605.2 1.3 maximum_maximum_fusion
  606.6 3.9 fusion.7
  610.7 0.8 copy.62
  611.7 1.9 convolution_add_fusion
  614.9 0.8 convolution_subtract_fusion.7
  617.3 0.8 convolution_subtract_fusion.5
  618.5 0.9 maximum_bitcast_fusion.1
  (175 shorter events, 28.3 us)
Async XLA Ops:
  7.2 236.2 %all-reduce.5.cloned.1.call-start = ((), (), s32[]{:S(2)}) async-start(), calls=%async_computation | async-start | bytes 3276800 | tf_op jit(solution)/shard_map/psum | solution.py:45
  69.9 36.1 %copy-start.15 = (s32[1,1,5]{2,1,0:T(1,128)S(1)}, s32[1,1,5]{2,1,0:T(1,128)}, u32[]{:S(2)}) copy-start(s32[1,1,5]{2,1,0:T(1,128)} %param.17) | copy-start | bytes 64
  69.9 36.2 %copy-start.7 = (f32[1,1,384,640]{3,2,1,0:T(8,128)S(1)}, f32[1,1,384,640]{3,2,1,0:T(8,128)}, u32[]{:S(2)}) copy-start(f32[1,1,384,640]{3,2,1,0:T(8,128)} %param.16) | copy-start | bytes 2949124
  106.0 2.2 copy-start.4
  107.1 1.6 copy-start.11
  108.6 9.2 %copy-start = (f32[128,640]{1,0:T(8,128)}, f32[128,640]{1,0:T(8,128)S(1)}, u32[]{:S(2)}) copy-start(f32[128,640]{1,0:T(8,128)S(1)} %fusion.75) | copy-start | bytes 983044
  117.8 0.7 copy-start.13
  117.8 376.9 %all-reduce.7.cloned.1.call-start = ((), (), s32[]{:S(2)}) async-start(), calls=%async_computation.1 | async-start | bytes 1179648 | tf_op jit(solution)/shard_map/psum | solution.py:61
  319.6 1.0 copy-start.10
  319.6 175.1 %copy-start.12 = (f32[384]{0:T(512)S(1)}, f32[384]{0:T(512)}, u32[]{:S(2)}) copy-start(f32[384]{0:T(512)} %param.20) | copy-start | bytes 4612
  494.7 1.4 copy-start.3
  531.0 22.6 %copy-start.14 = (f32[128]{0:T(128)S(1)}, f32[128]{0:T(128)}, u32[]{:S(2)}) copy-start(f32[128]{0:T(128)} %get-tuple-element.124) | copy-start | bytes 1540
  557.5 37.0 %copy-start.6 = (f32[384,384]{0,1:T(8,128)S(1)}, f32[384,384]{0,1:T(8,128)}, u32[]{:S(2)}) copy-start(f32[384,384]{0,1:T(8,128)} %fusion.23) | copy-start | bytes 1769476
  602.4 1.1 copy-start.9
  605.2 1.3 copy-start.1
  605.2 1.4 copy-start.2
  610.5 1.2 copy-start.8
  610.7 3.0 copy-start.5
Sparse Core Ops, SparseCore 0:
  118.0 125.3 all-reduce.4
  320.7 173.9 all-reduce.6
where the time goes:
time: 636 us; the launch traced here: 627 us
  waiting for transfers between devices  293 us (46%)
  other arithmetic  237 us (37%)
  local copies, waits for them, and re-layouts  40.4 us (6%)
  matrix products  35.5 us (6%)
  between operations  20.6 us (3%)
    psum x1, waiting for transfers between devices, body(): total = lax.psum(national_part, 'region')  173 us
    psum x1, waiting for transfers between devices, body(): complement_matrix = lax.psum(placed - term, 'dev')  120 us
    another operation x9, other arithmetic, upper_solve(): lax.linalg.triangular_solve(chol, right, left_side=True, lower=True, tran...  78.8 us
    another operation x11, other arithmetic, body(): chol_n = jnp.linalg.cholesky(normal_mat)  57.5 us
    another operation x10, other arithmetic, body(): chol = jnp.linalg.cholesky(interior[0, 0])  56.6 us
    another operation x7, other arithmetic, body(): eliminated_factor = jnp.linalg.cholesky(eliminated_rows)  34.5 us
  transfers between devices with their start and end apart: 2, of which 2 were waited for; matrix products, arithmetic and copies ran while one was open for 1% of the time, Pallas kernels for 0%

commit v1 on v0

v1 whole, which is shorter than its diff:
```python
import functools

import jax
import jax.numpy as jnp
from jax import lax
from jax.experimental import pallas as pl
from jax.experimental.pallas import tpu as pltpu
from jax.sharding import PartitionSpec as P

NI = 384
NE = 256
NS = 384
NRC = 640
TILE = 128
EXACT = lax.Precision.HIGHEST
F32 = jnp.float32
VMEM = pltpu.VMEM


def dot(a, b, dims=((1,), (0,))):
    return lax.dot_general(a, b, (dims, ((), ())), precision=EXACT, preferred_element_type=F32)


def split3(x):
    h = x.astype(jnp.bfloat16)
    rest = x - h.astype(F32)
    m = rest.astype(jnp.bfloat16)
    return h, m, (rest - m.astype(F32)).astype(jnp.bfloat16)


def select_right(x, onehot, dims=((1,), (0,))):
    h, m, l = (lax.dot_general(part, onehot, (dims, ((), ())), preferred_element_type=F32) for part in split3(x))
    return (h + m) + l


def select_left(onehot, x, dims=((1,), (0,))):
    h, m, l = (lax.dot_general(onehot, part, (dims, ((), ())), preferred_element_type=F32) for part in split3(x))
    return (h + m) + l


def row(x, k):
    return jnp.broadcast_to(x[k : k + 1, :], (8, 128))


def col(x, k):
    return jnp.broadcast_to(x[:, k : k + 1], (8, 128))


def recip(x):
    r = pl.reciprocal(x, approx=True)
    r = r * (2.0 - x * r)
    return r * (2.0 - x * r)


def inverse8(c, sub):
    c = list(c)
    for k in range(0, 8, 2):
        k1 = k + 1
        a, b, b2, e = row(c[k], k), row(c[k1], k), row(c[k], k1), row(c[k1], k1)
        rd = recip(a * e - b * b2)
        ia, ib, ib2, ie = e * rd, -(b * rd), -(b2 * rd), a * rd
        r0, r1 = sub == k, sub == k1
        ck, ck1 = c[k], c[k1]
        for j in range(8):
            if j in (k, k1):
                continue
            x, y = row(c[j], k), row(c[j], k1)
            m0, m1 = ia * x + ib * y, ib2 * x + ie * y
            c[j] = jnp.where(r0, m0, jnp.where(r1, m1, c[j] - (ck * m0 + ck1 * m1)))
        c[k] = jnp.where(r0, ia, jnp.where(r1, ib2, -(ck * ia + ck1 * ib2)))
        c[k1] = jnp.where(r0, ib, jnp.where(r1, ie, -(ck * ib + ck1 * ie)))
    return c


def sum8(t):
    return ((t[0] + t[1]) + (t[2] + t[3])) + ((t[4] + t[5]) + (t[6] + t[7]))


def inverse128(a):
    a = list(a)
    n = len(a)
    sub = lax.broadcasted_iota(jnp.int32, (8, 128), 0)
    lane = lax.broadcasted_iota(jnp.int32, (8, 128), 1)
    for p in range(n):
        lo = 8 * p
        r = a[p]
        d = inverse8([col(r, lo + j) for j in range(8)], sub)
        u = sum8([d[j] * row(r, j) for j in range(8)])
        for j in range(8):
            u = jnp.where(lane == lo + j, d[j], u)
        inside = (lane >= lo) & (lane < lo + 8)
        rows = [row(u, j) for j in range(8)]
        for step in range(n - 1):
            i = (p + 1 + step) % n
            x = a[i]
            a[i] = jnp.where(inside, 0.0, x) - sum8([col(x, lo + j) * rows[j] for j in range(8)])
        a[p] = u
    return a


def invert(w, blocks):
    def step(k, _):
        at = pl.ds(pl.multiple_of(k * TILE, TILE), TILE)
        full = w[at, at]
        pivot = jnp.concatenate(inverse128([full[8 * i : 8 * i + 8, :] for i in range(TILE // 8)]), axis=0)
        column = w[:, at]
        w[at, at] = jnp.zeros((TILE, TILE), F32)
        scaled = dot(pivot, w[at, :])
        w[:, at] = jnp.zeros((blocks * TILE, TILE), F32)
        w[...] = w[...] - dot(column, scaled)
        w[:, at] = -dot(column, pivot)
        w[at, :] = scaled
        w[at, at] = pivot
        return 0

    lax.fori_loop(0, blocks, step, 0)


def national(sep_row):
    return (lax.broadcasted_iota(jnp.int32, (NS, NS), 0) == sep_row).astype(jnp.bfloat16)


def first_kernel(mask, interior, coupling, prior, sep, own_row, ainv, gain, ec, ss):
    ainv[...] = interior[...]
    invert(ainv, NI // TILE)
    perm = national(sep[...])
    m_e = jnp.concatenate([coupling[:, TILE * t : TILE * (t + 1)] * mask[0, t].astype(F32) for t in range(2)], axis=1)
    m_s = jnp.concatenate([coupling[:, TILE * t : TILE * (t + 1)] * mask[0, t].astype(F32) for t in range(2, 5)], axis=1)
    m_s = select_right(m_s, perm, ((1,), (1,)))
    g_e = dot(ainv[...], m_e)
    g_s = dot(ainv[...], m_s)
    gain[:, :NE] = g_e
    gain[:, NE:] = g_s
    place = (lax.broadcasted_iota(jnp.int32, (NRC, own_row.shape[1]), 0) == own_row[...]).astype(jnp.bfloat16)
    p_s = select_right(prior[:, NE:], perm, ((1,), (1,)))
    ec[:, :NE] = select_left(place[:NE], prior[:, :NE]) - dot(m_e, g_e, ((0,), (0,)))
    ec[:, NE:] = select_left(place[:NE], p_s) - dot(m_e, g_s, ((0,), (0,)))
    ss[...] = select_left(place[NE:], p_s) - dot(m_s, g_s, ((0,), (0,)))


def second_kernel(ec, ss_own, own24, einv, weights, reduced_own):
    einv[...] = ec[:, :NE]
    invert(einv, NE // TILE)
    cross = ec[:, NE:]
    w = dot(einv[...], cross)
    weights[...] = w
    pick = (lax.broadcasted_iota(jnp.int32, (ss_own.shape[0], NS), 1) == own24[...]).astype(jnp.bfloat16)
    reduced_own[...] = ss_own[...] - dot(select_left(pick, cross, ((1,), (1,))), w)


def third_kernel(total, diag, sep, own_col, ainv, gain, einv, weights, out, rows, normal, h):
    i0 = lax.broadcasted_iota(jnp.int32, (NS, NS), 0)
    i1 = lax.broadcasted_iota(jnp.int32, (NS, NS), 1)
    normal[...] = total[...] + jnp.where(i0 == i1, diag[...], 0.0)
    invert(normal, NS // TILE)
    x = normal[...]
    w = weights[...]
    g_e = gain[:, :NE]
    h[...] = gain[:, NE:] - dot(g_e, w)
    base = ainv[...] + dot(dot(g_e, einv[...]), g_e, ((1,), (1,)))
    out[...] = base + dot(dot(h[...], x), h[...], ((1,), (1,)))
    count = own_col.shape[0]
    pick_e = (lax.broadcasted_iota(jnp.int32, (count, NE), 1) == own_col[...]).astype(jnp.bfloat16)
    pick_s = (lax.broadcasted_iota(jnp.int32, (count, NS), 1) + NE == own_col[...]).astype(F32)
    b_rows = pick_s - select_left(pick_e, w)
    t = dot(b_rows, x)
    rows[:, :NE] = select_left(pick_e, einv[...]) - dot(t, w, ((1,), (1,)))
    rows[:, NE:] = select_right(t, national(sep[...]))


def body(interior, coupling, tile_mask, prior, sep_map, nat_diag):
    dev_count = lax.axis_size("dev")
    own = lax.axis_index("dev")
    count = NRC // dev_count
    share = NS // dev_count
    sds = lambda *shape: jax.ShapeDtypeStruct(shape, F32)
    v = pl.BlockSpec(memory_space=VMEM)
    s = pl.BlockSpec(memory_space=pltpu.SMEM)
    where = jnp.concatenate([jnp.arange(NE, dtype=jnp.int32), sep_map[0] + NE])
    own_map = lax.dynamic_slice_in_dim(where, own * count, count, 0)
    own24 = (own * share + jnp.arange(share, dtype=jnp.int32))[:, None]
    ainv, gain, ec, ss = pl.pallas_call(
        first_kernel,
        out_shape=(sds(NI, NI), sds(NI, NRC), sds(NE, NRC), sds(NS, NS)),
        in_specs=[s, v, v, v, v, v],
        out_specs=(v, v, v, v),
    )(tile_mask[0], interior[0, 0], coupling[0, 0], prior[0], sep_map, own_map[None, :])
    ec, ss = lax.psum((ec, ss), "dev")
    ss_own = lax.dynamic_slice_in_dim(ss, own * share, share, 0)
    einv, weights, reduced_own = pl.pallas_call(
        second_kernel,
        out_shape=(sds(NE, NE), sds(NE, NS), sds(share, NS)),
        in_specs=[v, v, v],
        out_specs=(v, v, v),
    )(ec, ss_own, own24)
    total = lax.all_gather(lax.psum(reduced_own, "region"), "dev", axis=0, tiled=True)
    result, rows = pl.pallas_call(
        third_kernel,
        out_shape=(sds(NI, NI), sds(count, NRC)),
        in_specs=[v] * 8,
        out_specs=(v, v),
        scratch_shapes=[VMEM((NS, NS), F32), VMEM((NI, NS), F32)],
    )(total, nat_diag[None, :], sep_map, own_map[:, None], ainv, gain, einv, weights)
    return (result[None, None], rows[None])


def solution(mesh):
    placed = (
        P("region", "dev", None, None),
        P("region", "dev", None, None),
        P("region", "dev", None),
        P("region", "dev", None),
        P("region", None),
        P(),
    )
    return jax.shard_map(
        body,
        mesh=mesh,
        in_specs=placed,
        out_specs=(P("region", "dev", None, None), P("region", "dev", None)),
        check_vma=False,
    )
```

time: 636 us -> 322 us (0.51)
  the two profiles are of different devices: /device:TPU:2 before, /device:TPU:1 now
where the time goes in v1:
time: 322 us; the launch traced here: 321 us
  waiting for transfers between devices  127 us (39%)
  blocking collectives  105 us (33%)
  Pallas kernels  70.4 us (22%)
  between operations  14.1 us (4%)
  local copies, waits for them, and re-layouts  3.87 us (1%)
    psum x1, waiting for transfers between devices, body(): ec, ss = lax.psum((ec, ss), 'dev')  127 us
    psum x1, blocking collectives, body(): lax.psum(reduced_own, 'region')  69 us
    all_gather x1, blocking collectives, body(): lax.all_gather(lax.psum(reduced_own, 'region'), 'dev', axis=0, tiled=True)  36.2 us
    pallas_call x1, Pallas kernels, body(): pl.pallas_call(third_kernel, out_shape=(sds(NI, NI), sds(count, NRC)), in...  27.7 us
    pallas_call x1, Pallas kernels, body(): pl.pallas_call(first_kernel, out_shape=(sds(NI, NI), sds(NI, NRC), sds(NE...  27.1 us
    pallas_call x1, Pallas kernels, body(): pl.pallas_call(second_kernel, out_shape=(sds(NE, NE), sds(NE, NS), sds(sh...  15.6 us
  transfers between devices with their start and end apart: 1, of which 1 were waited for; matrix products, arithmetic and copies ran while one was open for 1% of the time, Pallas kernels for 0%

profile of v1, /device:TPU:1, one launch (start us, length us, event | category | flops | bytes accessed | tf_op | source)
XLA Modules:
  0.0 321.3 jit_solution(10614698222239349188)
XLA Ops:
  7.2 0.0 all-reduce.3.cloned.1.call-start
  7.2 0.0 copy-start
  7.2 0.7 copy-done
  7.9 0.6 dynamic-slice_bitcast_fusion
  8.5 27.1 %shard_map.77 = (f32[384,384]{1,0:T(8,128)}, f32[384,640]{1,0:T(8,128)}, f32[256,640]{1,0:T(8,128)}, f32[384,384]{1,0:T(8,128)}) custom-call(s32[1,5]{1,0:T(1,128)} %bitcast.13, f32[384,384]{1,0:T(8,128)} %bitcast.11, f32[384,640]{1,0:T(8,128)} %bitcast.10, f32[40,640]{1,0:T(8,128)} %bitcast.12, s32[1,384]{1,0:T(1,128)} %sep.3, ...), custom_call_target="tpu_custom_call" | custom-call | tf_op jit(solution)/shard_map/pallas_call | solution.py:182
  35.6 0.0 all-reduce.3.cloned.1.call-update
  35.6 0.0 copy-start.1
  35.6 0.7 copy.8.own_col
  36.3 0.0 copy-done.1
  36.3 0.5 broadcast_in_dim.17.diag
  36.8 0.6 iota_add_fusion.own24
  37.4 127.1 %all-reduce.3.cloned.1.call-done = (f32[256,640]{1,0:T(8,128)}, f32[384,384]{1,0:T(8,128)}) async-done(((f32[256,640]{1,0:T(8,128)}, f32[384,384]{1,0:T(8,128)}), (f32[256,640]{1,0:T(8,128)}, f32[384,384]{1,0:T(8,128)})) %all-reduce.3.cloned.1.call-update) | async-done | bytes 1245200 | tf_op jit(solution)/shard_map/psum | solution.py:188
  164.6 1.4 constant_dynamic-slice_fusion.ss_own
  165.9 15.6 %shard_map.78 = (f32[256,256]{1,0:T(8,128)}, f32[256,384]{1,0:T(8,128)}, f32[24,384]{1,0:T(8,128)}) custom-call(f32[256,640]{1,0:T(8,128)} %get-tuple-element.20.ec, f32[24,384]{1,0:T(8,128)} %constant_dynamic-slice_fusion.ss_own, s32[24,1]{1,0:T(8,128)} %iota_add_fusion.own24), custom_call_target="tpu_custom_call" | custom-call | tf_op jit(solution)/shard_map/pallas_call | solution.py:190
  181.6 69.0 %psum.23 = f32[24,384]{1,0:T(8,128)S(1)} all-reduce(f32[24,384]{1,0:T(8,128)} %get-tuple-element.13), channel_id=1, replica_groups=mesh['region'=16,'dev'=16] {'region'}, use_global_device_ids=true, to_apply=%region_2.0 | all-reduce | flops 9216 | bytes 73728 | tf_op jit(solution)/shard_map/psum | solution.py:196
  250.6 36.2 %all_gather.3.total = f32[384,384]{1,0:T(8,128)} all-gather(f32[24,384]{1,0:T(8,128)S(1)} %psum.23), channel_id=1, replica_groups=mesh['region'=16,'dev'=16] {'dev'}, dimensions={0}, use_global_device_ids=true | all-gather | bytes 626688 | tf_op jit(solution)/shard_map/all_gather | solution.py:196
  286.7 27.7 %shard_map.79 = (f32[384,384]{1,0:T(8,128)}, f32[40,640]{1,0:T(8,128)}) custom-call(f32[384,384]{1,0:T(8,128)} %all_gather.3.total, f32[1,384]{1,0:T(1,128)} %broadcast_in_dim.17.diag, s32[1,384]{1,0:T(1,128)} %sep.3, s32[40,1]{1,0:T(8,128)} %copy.8.own_col, f32[384,384]{1,0:T(8,128)} %get-tuple-element.14.ainv, f32[384,640]{1,0:T(8,128)} %get-tuple-element.15.gain, ...), custom_call_target="tpu_custom_call" | custom-call | tf_op jit(solution)/shard_map/pallas_call | solution.py:197
  (3 shorter events, 0.0 us)
Async XLA Ops:
  7.2 157.4 %all-reduce.3.cloned.1.call-start = ((), (), s32[]{:S(2)}) async-start(), calls=%async_computation | async-start | bytes 2490368 | tf_op jit(solution)/shard_map/psum | solution.py:188
  7.2 0.7 copy-start
  35.6 0.7 copy-start.1
Sparse Core Ops, SparseCore 0:
  35.7 128.7 all-reduce.2

commit v2 on v1

--- a/solution.py
+++ b/solution.py
@@ -15,6 +15,7 @@
 EXACT = lax.Precision.HIGHEST
 F32 = jnp.float32
 VMEM = pltpu.VMEM
+MESH = pl.DeviceIdType.MESH
 
 
 def dot(a, b, dims=((1,), (0,))):
@@ -138,27 +139,133 @@
     ss[...] = select_left(place[NE:], p_s) - dot(m_s, g_s, ((0,), (0,)))
 
 
-def second_kernel(ec, ss_own, own24, einv, weights, reduced_own):
-    einv[...] = ec[:, :NE]
+def second_kernel(
+    ec, ss, ainv, gain, own24, total, einv, weights, base, h,
+    half_e, half_x, half_s, acc_e, acc_x, acc_s, rs_e, rs_x, rs_s, e_all, x_all, y_all, z_all, n_all,
+    half_sem, rs_sem, ag_sem, reg_sem, send_sem,
+):
+    me, region = lax.axis_index("dev"), lax.axis_index("region")
+    q, core = lax.div(me, 2), lax.rem(me, 2)
+    y, z = lax.div(region, 4), lax.rem(region, 4)
+    place = core * 8 + q
+    sent = []
+
+    def send(src, dst, recv, **where):
+        copy = pltpu.make_async_remote_copy(
+            src_ref=src, dst_ref=dst, send_sem=send_sem.at[len(sent)], recv_sem=recv,
+            device_id=where, device_id_type=MESH,
+        )
+        copy.start()
+        sent.append(copy)
+
+    def arrived(dst, recv):
+        pltpu.make_async_remote_copy(
+            src_ref=dst, dst_ref=dst, send_sem=send_sem.at[0], recv_sem=recv,
+            device_id={"dev": lax.rem(me + 1, 16)}, device_id_type=MESH,
+        ).wait_recv()
+
+    others = [lax.rem(me + t, 16) for t in range(1, 16)]
+    same_core = [lax.rem(q + t, 8) for t in range(1, 8)]
+    y_peers = [lax.rem(y + t, 4) for t in range(1, 4)]
+    z_peers = [lax.rem(z + t, 4) for t in range(1, 4)]
+
+    barrier = pltpu.get_barrier_semaphore()
+    for other in others:
+        pl.semaphore_signal(barrier, inc=1, device_id={"dev": other}, device_id_type=MESH)
+    for other in y_peers:
+        pl.semaphore_signal(barrier, inc=1, device_id={"region": other * 4 + z}, device_id_type=MESH)
+    for other in z_peers:
+        pl.semaphore_signal(barrier, inc=1, device_id={"region": y * 4 + other}, device_id_type=MESH)
+    pl.semaphore_wait(barrier, 21)
+
+    partner = q * 2 + (1 - core)
+    away, home = 1 - core, core
+    ec_rows = lambda at: pl.ds(pl.multiple_of(at * 128, 128), 128)
+    ss_rows = lambda at: pl.ds(pl.multiple_of(at * 192, 192), 192)
+    parts = (
+        (ec.at[ec_rows(away), pl.ds(0, NE)], half_e),
+        (ec.at[ec_rows(away), pl.ds(NE, NS)], half_x),
+        (ss.at[ss_rows(away), :], half_s),
+    )
+    for n, (src, dst) in enumerate(parts):
+        send(src, dst, half_sem.at[n], dev=partner)
+
+    def scatter(kind, acc, slots, size):
+        for other in same_core:
+            rows = pl.ds(pl.multiple_of(other * size, size), size)
+            send(acc.at[rows, :], slots.at[q], rs_sem.at[kind, q], dev=other * 2 + core)
+
+    def gathered(kind, acc, slots, size):
+        value = acc[pl.ds(pl.multiple_of(q * size, size), size), :]
+        for other in same_core:
+            arrived(slots.at[other], rs_sem.at[kind, other])
+            value = value + slots[other]
+        return value
+
+    def rows_of(dev, size):
+        return pl.ds(pl.multiple_of((lax.rem(dev, 2) * 8 + lax.div(dev, 2)) * size, size), size)
+
+    def spread(kind, full, size):
+        for other in others:
+            send(full.at[rows_of(me, size), :], full.at[rows_of(me, size), :], ag_sem.at[kind, me], dev=other)
+
+    def complete(kind, full, size):
+        for other in others:
+            arrived(full.at[rows_of(other, size), :], ag_sem.at[kind, other])
+
+    arrived(half_e, half_sem.at[0])
+    acc_e[...] = ec[ec_rows(home), :NE] + half_e[...]
+    scatter(0, acc_e, rs_e, 16)
+    arrived(half_x, half_sem.at[1])
+    acc_x[...] = ec[ec_rows(home), NE:] + half_x[...]
+    scatter(1, acc_x, rs_x, 16)
+    e_all[rows_of(me, 16), :] = gathered(0, acc_e, rs_e, 16)
+    spread(0, e_all, 16)
+    x_all[rows_of(me, 16), :] = gathered(1, acc_x, rs_x, 16)
+    spread(1, x_all, 16)
+    arrived(half_s, half_sem.at[2])
+    acc_s[...] = ss[ss_rows(home), :] + half_s[...]
+    scatter(2, acc_s, rs_s, 24)
+
+    complete(0, e_all, 16)
+    einv[...] = e_all[...]
     invert(einv, NE // TILE)
-    cross = ec[:, NE:]
+    complete(1, x_all, 16)
+    cross = x_all[...]
     w = dot(einv[...], cross)
     weights[...] = w
-    pick = (lax.broadcasted_iota(jnp.int32, (ss_own.shape[0], NS), 1) == own24[...]).astype(jnp.bfloat16)
-    reduced_own[...] = ss_own[...] - dot(select_left(pick, cross, ((1,), (1,))), w)
-
-
-def third_kernel(total, diag, sep, own_col, ainv, gain, einv, weights, out, rows, normal, h):
+    pick = (lax.broadcasted_iota(jnp.int32, (24, NS), 1) == own24[...]).astype(jnp.bfloat16)
+    own = gathered(2, acc_s, rs_s, 24) - dot(select_left(pick, cross, ((1,), (1,))), w)
+
+    y_all[y] = own
+    for other in y_peers:
+        send(y_all.at[y], y_all.at[y], reg_sem.at[0, y], region=other * 4 + z)
+    g_e = gain[:, :NE]
+    h[...] = gain[:, NE:] - dot(g_e, w)
+    for other in y_peers:
+        arrived(y_all.at[other], reg_sem.at[0, other])
+    z_all[z] = (y_all[0] + y_all[1]) + (y_all[2] + y_all[3])
+    for other in z_peers:
+        send(z_all.at[z], z_all.at[z], reg_sem.at[1, z], region=y * 4 + other)
+    base[...] = ainv[...] + dot(dot(g_e, einv[...]), g_e, ((1,), (1,)))
+    for other in z_peers:
+        arrived(z_all.at[other], reg_sem.at[1, other])
+    n_all[rows_of(me, 24), :] = (z_all[0] + z_all[1]) + (z_all[2] + z_all[3])
+    spread(2, n_all, 24)
+    complete(2, n_all, 24)
+    total[...] = n_all[...]
+    for copy in sent:
+        copy.wait_send()
+
+
+def third_kernel(total, diag, sep, own_col, base, h, einv, weights, out, rows, normal):
     i0 = lax.broadcasted_iota(jnp.int32, (NS, NS), 0)
     i1 = lax.broadcasted_iota(jnp.int32, (NS, NS), 1)
     normal[...] = total[...] + jnp.where(i0 == i1, diag[...], 0.0)
     invert(normal, NS // TILE)
     x = normal[...]
     w = weights[...]
-    g_e = gain[:, :NE]
-    h[...] = gain[:, NE:] - dot(g_e, w)
-    base = ainv[...] + dot(dot(g_e, einv[...]), g_e, ((1,), (1,)))
-    out[...] = base + dot(dot(h[...], x), h[...], ((1,), (1,)))
+    out[...] = base[...] + dot(dot(h[...], x), h[...], ((1,), (1,)))
     count = own_col.shape[0]
     pick_e = (lax.broadcasted_iota(jnp.int32, (count, NE), 1) == own_col[...]).astype(jnp.bfloat16)
     pick_s = (lax.broadcasted_iota(jnp.int32, (count, NS), 1) + NE == own_col[...]).astype(F32)
@@ -178,29 +285,36 @@
     s = pl.BlockSpec(memory_space=pltpu.SMEM)
     where = jnp.concatenate([jnp.arange(NE, dtype=jnp.int32), sep_map[0] + NE])
     own_map = lax.dynamic_slice_in_dim(where, own * count, count, 0)
-    own24 = (own * share + jnp.arange(share, dtype=jnp.int32))[:, None]
+    place = (own % 2) * (dev_count // 2) + own // 2
+    own24 = (place * share + jnp.arange(share, dtype=jnp.int32))[:, None]
     ainv, gain, ec, ss = pl.pallas_call(
         first_kernel,
         out_shape=(sds(NI, NI), sds(NI, NRC), sds(NE, NRC), sds(NS, NS)),
         in_specs=[s, v, v, v, v, v],
         out_specs=(v, v, v, v),
     )(tile_mask[0], interior[0, 0], coupling[0, 0], prior[0], sep_map, own_map[None, :])
-    ec, ss = lax.psum((ec, ss), "dev")
-    ss_own = lax.dynamic_slice_in_dim(ss, own * share, share, 0)
-    einv, weights, reduced_own = pl.pallas_call(
+    dma = pltpu.SemaphoreType.DMA
+    buf = lambda *shape: VMEM(shape, F32)
+    total, einv, weights, base, h = pl.pallas_call(
         second_kernel,
-        out_shape=(sds(NE, NE), sds(NE, NS), sds(share, NS)),
-        in_specs=[v, v, v],
-        out_specs=(v, v, v),
-    )(ec, ss_own, own24)
-    total = lax.all_gather(lax.psum(reduced_own, "region"), "dev", axis=0, tiled=True)
+        out_shape=(sds(NS, NS), sds(NE, NE), sds(NE, NS), sds(NI, NI), sds(NI, NS)),
+        in_specs=[v] * 5,
+        out_specs=(v,) * 5,
+        scratch_shapes=[
+            buf(128, NE), buf(128, NS), buf(192, NS), buf(128, NE), buf(128, NS), buf(192, NS),
+            buf(8, 16, NE), buf(8, 16, NS), buf(8, 24, NS), buf(NE, NE), buf(NE, NS),
+            buf(4, 24, NS), buf(4, 24, NS), buf(NS, NS),
+            dma((3,)), dma((3, 8)), dma((3, 16)), dma((2, 4)), dma((80,)),
+        ],
+        compiler_params=pltpu.CompilerParams(collective_id=0, has_side_effects=True),
+    )(ec, ss, ainv, gain, own24)
     result, rows = pl.pallas_call(
         third_kernel,
         out_shape=(sds(NI, NI), sds(count, NRC)),
         in_specs=[v] * 8,
         out_specs=(v, v),
-        scratch_shapes=[VMEM((NS, NS), F32), VMEM((NI, NS), F32)],
-    )(total, nat_diag[None, :], sep_map, own_map[:, None], ainv, gain, einv, weights)
+        scratch_shapes=[VMEM((NS, NS), F32)],
+    )(total, nat_diag[None, :], sep_map, own_map[:, None], base, h, einv, weights)
     return (result[None, None], rows[None])
 
 

time: 322 us -> 115 us (0.36)
  waiting for transfers between devices: 127 us -> 0 us
  blocking collectives: 105 us -> 0 us
  Pallas kernels: 70.4 us -> 111 us
  between operations: 14.1 us -> 0.68 us
    psum x1 -> x0, waiting for transfers between devices: 127 us -> none  [body(): ec, ss = lax.psum((ec, ss), 'dev')]
    psum x1 -> x0, blocking collectives: 69 us -> none  [body(): lax.psum(reduced_own, 'region')]
    pallas_call x1, Pallas kernels: 15.6 us -> 58.4 us  [body(): pl.pallas_call(second_kernel, out_shape=(sds(NS, NS), sds(NE, NE), sds(NE...]
    all_gather x1 -> x0, blocking collectives: 36.2 us -> none  [body(): lax.all_gather(lax.psum(reduced_own, 'region'), 'dev', axis=0, tiled=True)]
  transfers between devices with their start and end apart: 1 -> 0, of which waited for: 1 -> 0; matrix products, arithmetic and copies ran while one was open for 1% -> 0% of each run, Pallas kernels for 0% -> 0%
where the time goes in v2:
time: 115 us
  Pallas kernels  111 us (97%)
  local copies, waits for them, and re-layouts  2.57 us (2%)
    pallas_call x1, Pallas kernels, body(): pl.pallas_call(second_kernel, out_shape=(sds(NS, NS), sds(NE, NE), sds(NE...  58.4 us
    pallas_call x1, Pallas kernels, body(): pl.pallas_call(first_kernel, out_shape=(sds(NI, NI), sds(NI, NRC), sds(NE...  27.1 us
    pallas_call x1, Pallas kernels, body(): pl.pallas_call(third_kernel, out_shape=(sds(NI, NI), sds(count, NRC)), in...  25.5 us

profile of v2, /device:TPU:1, one launch (start us, length us, event | category | flops | bytes accessed | tf_op | source)
XLA Modules:
  0.0 114.9 jit_solution(14021917261527811373)
XLA Ops:
  0.7 0.6 iota_add_fusion.own24
  1.3 0.0 copy-start
  1.3 0.7 copy-done
  2.0 0.6 dynamic-slice_bitcast_fusion
  2.6 27.1 %shard_map.77 = (f32[384,384]{1,0:T(8,128)}, f32[384,640]{1,0:T(8,128)}, f32[256,640]{1,0:T(8,128)}, f32[384,384]{1,0:T(8,128)}) custom-call(s32[1,5]{1,0:T(1,128)} %bitcast.13, f32[384,384]{1,0:T(8,128)} %bitcast.11, f32[384,640]{1,0:T(8,128)} %bitcast.10, f32[40,640]{1,0:T(8,128)} %bitcast.12, s32[1,384]{1,0:T(1,128)} %sep.3, ...), custom_call_target="tpu_custom_call" | custom-call | tf_op jit(solution)/shard_map/pallas_call | solution.py:290
  29.7 58.4 %shard_map.78 = (f32[384,384]{1,0:T(8,128)}, f32[256,256]{1,0:T(8,128)}, f32[256,384]{1,0:T(8,128)}, f32[384,384]{1,0:T(8,128)}, f32[384,384]{1,0:T(8,128)}) custom-call(f32[256,640]{1,0:T(8,128)} %get-tuple-element.13.ec, f32[384,384]{1,0:T(8,128)} %get-tuple-element.14.ss, f32[384,384]{1,0:T(8,128)} %get-tuple-element.15.ainv, ...), custom_call_target="tpu_custom_call" | custom-call | tf_op jit(solution)/shard_map/pallas_call | solution.py:298
  88.1 0.0 copy-start.1
  88.1 0.7 copy.8.own_col
  88.8 0.0 copy-done.1
  88.8 0.6 broadcast_in_dim.17.diag
  89.4 25.5 %shard_map.79 = (f32[384,384]{1,0:T(8,128)}, f32[40,640]{1,0:T(8,128)}) custom-call(f32[384,384]{1,0:T(8,128)} %get-tuple-element.17.total, f32[1,384]{1,0:T(1,128)} %broadcast_in_dim.17.diag, s32[1,384]{1,0:T(1,128)} %sep.3, s32[40,1]{1,0:T(8,128)} %copy.8.own_col, f32[384,384]{1,0:T(8,128)} %get-tuple-element.18.base, f32[384,384]{1,0:T(8,128)} %get-tuple-element.19.h, ...), custom_call_target="tpu_custom_call" | custom-call | tf_op jit(solution)/shard_map/pallas_call | solution.py:311
  (3 shorter events, 0.0 us)
Async XLA Ops:
  1.3 0.7 copy-start
  88.1 0.7 copy-start.1

commit v3 on v2

v3 whole, which is shorter than its diff:
```python
import jax
import jax.numpy as jnp
from jax import lax
from jax.experimental import pallas as pl
from jax.experimental.pallas import tpu as pltpu
from jax.sharding import PartitionSpec as P

NI = 384
NE = 256
NS = 384
NRC = 640
TILE = 128
EXACT = lax.Precision.HIGHEST
F32 = jnp.float32
VMEM = pltpu.VMEM
MESH = pl.DeviceIdType.MESH


def dot(a, b, dims=((1,), (0,))):
    return lax.dot_general(a, b, (dims, ((), ())), precision=EXACT, preferred_element_type=F32)


def fast(a, b, dims=((1,), (0,))):
    return lax.dot_general(a, b, (dims, ((), ())), precision=lax.Precision.HIGH, preferred_element_type=F32)


def rough(a, b):
    return lax.dot_general(
        a.astype(jnp.bfloat16), b.astype(jnp.bfloat16), (((1,), (0,)), ((), ())), preferred_element_type=F32
    )


def split3(x):
    h = x.astype(jnp.bfloat16)
    rest = x - h.astype(F32)
    m = rest.astype(jnp.bfloat16)
    return h, m, (rest - m.astype(F32)).astype(jnp.bfloat16)


def select_right(x, onehot, dims=((1,), (0,))):
    h, m, l = (lax.dot_general(part, onehot, (dims, ((), ())), preferred_element_type=F32) for part in split3(x))
    return (h + m) + l


def select_left(onehot, x, dims=((1,), (0,))):
    h, m, l = (lax.dot_general(onehot, part, (dims, ((), ())), preferred_element_type=F32) for part in split3(x))
    return (h + m) + l


def row(x, k):
    return jnp.broadcast_to(x[k : k + 1, :], (8, 128))


def col(x, k):
    return jnp.broadcast_to(x[:, k : k + 1], (8, 128))


def recip(x):
    r = pl.reciprocal(x, approx=True)
    r = r * (2.0 - x * r)
    return r * (2.0 - x * r)


def inverse8(c, sub):
    c = list(c)
    for k in range(0, 8, 2):
        k1 = k + 1
        a, b, b2, e = row(c[k], k), row(c[k1], k), row(c[k], k1), row(c[k1], k1)
        rd = recip(a * e - b * b2)
        ia, ib, ib2, ie = e * rd, -(b * rd), -(b2 * rd), a * rd
        r0, r1 = sub == k, sub == k1
        ck, ck1 = c[k], c[k1]
        for j in range(8):
            if j in (k, k1):
                continue
            x, y = row(c[j], k), row(c[j], k1)
            m0, m1 = ia * x + ib * y, ib2 * x + ie * y
            c[j] = jnp.where(r0, m0, jnp.where(r1, m1, c[j] - (ck * m0 + ck1 * m1)))
        c[k] = jnp.where(r0, ia, jnp.where(r1, ib2, -(ck * ia + ck1 * ib2)))
        c[k1] = jnp.where(r0, ib, jnp.where(r1, ie, -(ck * ib + ck1 * ie)))
    return c


def sum8(t):
    return ((t[0] + t[1]) + (t[2] + t[3])) + ((t[4] + t[5]) + (t[6] + t[7]))


def inverse128(a):
    a = list(a)
    n = len(a)
    sub = lax.broadcasted_iota(jnp.int32, (8, 128), 0)
    lane = lax.broadcasted_iota(jnp.int32, (8, 128), 1)
    for p in range(n):
        lo = 8 * p
        r = a[p]
        d = inverse8([col(r, lo + j) for j in range(8)], sub)
        u = sum8([d[j] * row(r, j) for j in range(8)])
        for j in range(8):
            u = jnp.where(lane == lo + j, d[j], u)
        inside = (lane >= lo) & (lane < lo + 8)
        rows = [row(u, j) for j in range(8)]
        for step in range(n - 1):
            i = (p + 1 + step) % n
            x = a[i]
            a[i] = jnp.where(inside, 0.0, x) - sum8([col(x, lo + j) * rows[j] for j in range(8)])
        a[p] = u
    return a


def invert(w, blocks):
    def step(k, _):
        at = pl.ds(pl.multiple_of(k * TILE, TILE), TILE)
        full = w[at, at]
        pivot = jnp.concatenate(inverse128([full[8 * i : 8 * i + 8, :] for i in range(TILE // 8)]), axis=0)
        column = w[:, at]
        w[at, at] = jnp.zeros((TILE, TILE), F32)
        scaled = dot(pivot, w[at, :])
        w[:, at] = jnp.zeros((blocks * TILE, TILE), F32)
        w[...] = w[...] - dot(column, scaled)
        w[:, at] = -dot(column, pivot)
        w[at, :] = scaled
        w[at, at] = pivot
        return 0

    lax.fori_loop(0, blocks, step, 0)


def verified_inverse(a, x, low, steps):
    n = a.shape[0]
    eye = jnp.where(
        lax.broadcasted_iota(jnp.int32, (n, n), 0) == lax.broadcasted_iota(jnp.int32, (n, n), 1), 1.0, 0.0
    )
    full = a[...]
    high = jnp.max(jnp.sum(jnp.abs(full), axis=0, keepdims=True), axis=1, keepdims=True)
    c = 2.0 / (low + high)
    rho = (high - low) / (low + high)
    scale = 2.0 / (2.0 - rho * rho)
    x[...] = (2.0 * c * scale) * eye - (c * c * scale) * full
    rho = rho * rho / (2.0 - rho * rho)
    for _ in range(steps):
        scale = 2.0 / (2.0 - rho * rho)
        now = x[...]
        x[...] = (now * 2.0 - rough(now, rough(full, now))) * scale
        rho = rho * rho / (2.0 - rho * rho)

    def more(state):
        count, size = state
        return jnp.logical_and(count < 12, jnp.logical_not(size <= 1e-3))

    def step(state):
        count, _ = state
        now = x[...]
        r = eye - fast(a[...], now)
        x[...] = now + rough(now, r)
        return count + 1, jnp.sum(r * r)

    lax.while_loop(more, step, (jnp.int32(0), jnp.float32(1.0)))
    now = x[...]
    r = eye - dot(a[...], now)
    x[...] = now + rough(now, r)

    @pl.when(jnp.logical_not(jnp.sum(r * r) <= 1e-6))
    def _():
        x[...] = a[...]
        invert(x, n // TILE)


def national(sep_row):
    return (lax.broadcasted_iota(jnp.int32, (NS, NS), 0) == sep_row).astype(jnp.bfloat16)


def first_kernel(interior, ainv):
    verified_inverse(interior, ainv, 0.5, 3)


def second_kernel(
    mask, ainv, coupling, prior, sep, total, einv, weights, base, h,
    e_own, x_own, s_own, half_e, half_x, half_s, acc_e, acc_x, acc_s, rs_e, rs_x, rs_s,
    e_all, x_all, y_all, z_all, n_all, half_sem, rs_sem, ag_sem, reg_sem, send_sem,
):
    me, region = lax.axis_index("dev"), lax.axis_index("region")
    q, core = lax.div(me, 2), lax.rem(me, 2)
    y, z = lax.div(region, 4), lax.rem(region, 4)
    sent = []

    def send(src, dst, recv, **where):
        copy = pltpu.make_async_remote_copy(
            src_ref=src, dst_ref=dst, send_sem=send_sem.at[len(sent)], recv_sem=recv,
            device_id=where, device_id_type=MESH,
        )
        copy.start()
        sent.append(copy)

    def arrived(dst, recv):
        pltpu.make_async_remote_copy(
            src_ref=dst, dst_ref=dst, send_sem=send_sem.at[0], recv_sem=recv,
            device_id={"dev": lax.rem(me + 1, 16)}, device_id_type=MESH,
        ).wait_recv()

    others = [lax.rem(me + t, 16) for t in range(1, 16)]
    same_core = [lax.rem(q + t, 8) for t in range(1, 8)]
    y_peers = [lax.rem(y + t, 4) for t in range(1, 4)]
    z_peers = [lax.rem(z + t, 4) for t in range(1, 4)]

    barrier = pltpu.get_barrier_semaphore()
    for other in others:
        pl.semaphore_signal(barrier, inc=1, device_id={"dev": other}, device_id_type=MESH)
    for other in y_peers:
        pl.semaphore_signal(barrier, inc=1, device_id={"region": other * 4 + z}, device_id_type=MESH)
    for other in z_peers:
        pl.semaphore_signal(barrier, inc=1, device_id={"region": y * 4 + other}, device_id_type=MESH)

    partner = q * 2 + (1 - core)
    away = pl.ds(pl.multiple_of((1 - core) * 64, 64), 64)
    home = pl.ds(pl.multiple_of(core * 64, 64), 64)

    def rows_of(dev):
        return pl.ds(pl.multiple_of(lax.rem(dev, 2) * 64 + lax.div(dev, 2) * 8, 8), 8)

    def halve(kind, mine, half):
        send(mine.at[away, :], half.at[:, :], half_sem.at[kind], dev=partner)

    def scatter(kind, mine, half, acc, slots):
        arrived(half, half_sem.at[kind])
        acc[...] = mine[home, :] + half[...]
        for other in same_core:
            rows = pl.ds(pl.multiple_of(other * 8, 8), 8)
            send(acc.at[rows, :], slots.at[q], rs_sem.at[kind, q], dev=other * 2 + core)

    def gathered(kind, acc, slots):
        value = acc[pl.ds(pl.multiple_of(q * 8, 8), 8), :]
        for other in same_core:
            arrived(slots.at[other], rs_sem.at[kind, other])
            value = value + slots[other]
        return value

    def spread(kind, full):
        for other in others:
            send(full.at[rows_of(me), :], full.at[rows_of(me), :], ag_sem.at[kind, me], dev=other)

    def complete(kind, full):
        for other in others:
            arrived(full.at[rows_of(other), :], ag_sem.at[kind, other])

    count = prior.shape[0]
    perm = national(sep[...])
    m_e = jnp.concatenate([coupling[:, TILE * t : TILE * (t + 1)] * mask[0, t].astype(F32) for t in range(2)], axis=1)
    g_e = fast(ainv[...], m_e)
    at = lax.broadcasted_iota(jnp.int32, (NE, count), 1) + me * count
    place_e = (lax.broadcasted_iota(jnp.int32, (NE, count), 0) == at).astype(jnp.bfloat16)
    p_e = select_left(place_e, prior[:, :NE])
    e_own[:, :TILE] = p_e[:TILE, :TILE] - dot(m_e[:, :TILE], g_e[:, :TILE], ((0,), (0,)))
    e_own[:, TILE:] = p_e[TILE:, :] - dot(m_e[:, TILE:], g_e, ((0,), (0,)))
    pl.semaphore_wait(barrier, 21)
    halve(0, e_own, half_e)

    m_s = jnp.concatenate([coupling[:, TILE * t : TILE * (t + 1)] * mask[0, t].astype(F32) for t in range(2, 5)], axis=1)
    m_s = select_right(m_s, perm, ((1,), (1,)))
    scatter(0, e_own, half_e, acc_e, rs_e)
    g_s = fast(ainv[...], m_s)
    p_s = select_right(prior[:, NE:], perm, ((1,), (1,)))
    p_x = select_left(place_e, p_s)
    x_term = dot(m_e, g_s, ((0,), (0,)))
    x_own[:, :NS] = p_x[:TILE] - x_term[:TILE]
    x_own[:, NS:] = p_x[TILE:] - x_term[TILE:]
    halve(1, x_own, half_x)
    e_all[rows_of(me), :] = gathered(0, acc_e, rs_e)
    spread(0, e_all)
    scatter(1, x_own, half_x, acc_x, rs_x)
    at = lax.broadcasted_iota(jnp.int32, (NS, count), 1) + (me * count - NE)
    local = (lax.broadcasted_iota(jnp.int32, (NS, count), 0) == at).astype(jnp.bfloat16)
    place_s = lax.dot_general(perm, local, (((1,), (0,)), ((), ())), preferred_element_type=F32).astype(jnp.bfloat16)
    p_s = select_left(place_s, p_s)
    s_own[:, :TILE] = p_s[:TILE, :TILE] - dot(m_s[:, :TILE], g_s[:, :TILE], ((0,), (0,)))
    s_own[:, TILE : 3 * TILE] = p_s[TILE:NE, :NE] - dot(m_s[:, TILE:NE], g_s[:, :NE], ((0,), (0,)))
    s_own[:, 3 * TILE :] = p_s[NE:, :] - dot(m_s[:, NE:], g_s, ((0,), (0,)))
    halve(2, s_own, half_s)
    x_all[rows_of(me), :] = gathered(1, acc_x, rs_x)
    spread(1, x_all)
    scatter(2, s_own, half_s, acc_s, rs_s)

    complete(0, e_all)
    einv[:TILE, :TILE] = e_all[:, :TILE]
    einv[TILE:, :] = e_all[:, TILE:]
    einv[:TILE, TILE:] = e_all[:, TILE:NE].T
    invert(einv, NE // TILE)
    complete(1, x_all)
    cross = jnp.concatenate([x_all[:, :NS], x_all[:, NS:]], axis=0)
    w = dot(einv[...], cross)
    weights[...] = w
    i0, i1 = (lax.broadcasted_iota(jnp.int32, (24, NS), d) for d in (0, 1))
    pick = (i1 == lax.div(i0, 8) * TILE + lax.rem(i0, 8) + core * 64 + q * 8).astype(jnp.bfloat16)
    part = dot(select_left(pick, cross, ((1,), (1,))), w)
    part = jnp.concatenate([part[:8, :TILE], part[8:16, :NE], part[16:, :]], axis=1)

    y_all[y] = gathered(2, acc_s, rs_s) - part
    for other in y_peers:
        send(y_all.at[y], y_all.at[y], reg_sem.at[0, y], region=other * 4 + z)
    h[...] = g_s - dot(g_e, w)
    for other in y_peers:
        arrived(y_all.at[other], reg_sem.at[0, other])
    z_all[z] = (y_all[0] + y_all[1]) + (y_all[2] + y_all[3])
    for other in z_peers:
        send(z_all.at[z], z_all.at[z], reg_sem.at[1, z], region=y * 4 + other)
    base[...] = ainv[...] + fast(dot(g_e, einv[...]), g_e, ((1,), (1,)))
    for other in z_peers:
        arrived(z_all.at[other], reg_sem.at[1, other])
    n_all[rows_of(me), :] = (z_all[0] + z_all[1]) + (z_all[2] + z_all[3])
    spread(2, n_all)
    complete(2, n_all)
    total[...] = n_all[...]
    for copy in sent:
        copy.wait_send()


def third_kernel(total, diag, sep, base, h, einv, weights, out, rows, normal, inverse):
    me = lax.axis_index("dev")
    t0, t1, t2 = total[:, :TILE], total[:, TILE : 3 * TILE], total[:, 3 * TILE :]
    normal[:TILE, :TILE] = t0
    normal[TILE:NE, :NE] = t1
    normal[NE:, :] = t2
    normal[:TILE, TILE:NE] = t1[:, :TILE].T
    normal[:TILE, NE:] = t2[:, :TILE].T
    normal[TILE:NE, NE:] = t2[:, TILE:NE].T
    i0, i1 = (lax.broadcasted_iota(jnp.int32, (NS, NS), d) for d in (0, 1))
    normal[...] = normal[...] + jnp.where(i0 == i1, diag[...], 0.0)
    verified_inverse(normal, inverse, 0.25, 2)
    x = inverse[...]
    w = weights[...]
    out[...] = base[...] + fast(fast(h[...], x), h[...], ((1,), (1,)))
    count = rows.shape[0]
    perm = national(sep[...])
    at = lambda n: lax.broadcasted_iota(jnp.int32, (count, n), 0) + me * count
    pick_e = (lax.broadcasted_iota(jnp.int32, (count, NE), 1) == at(NE)).astype(jnp.bfloat16)
    pick_s = (lax.broadcasted_iota(jnp.int32, (count, NS), 1) + NE == at(NS)).astype(jnp.bfloat16)
    pick_s = lax.dot_general(pick_s, perm, (((1,), (1,)), ((), ())), preferred_element_type=F32)
    t = dot(pick_s - select_left(pick_e, w), x)
    rows[:, :NE] = select_left(pick_e, einv[...]) - dot(t, w, ((1,), (1,)))
    rows[:, NE:] = select_right(t, perm)


def body(interior, coupling, tile_mask, prior, sep_map, nat_diag):
    count = prior.shape[1]
    sds = lambda *shape: jax.ShapeDtypeStruct(shape, F32)
    v = pl.BlockSpec(memory_space=VMEM)
    s = pl.BlockSpec(memory_space=pltpu.SMEM)
    dma = pltpu.SemaphoreType.DMA
    buf = lambda *shape: VMEM(shape, F32)
    ainv = pl.pallas_call(first_kernel, out_shape=sds(NI, NI), in_specs=[v], out_specs=v)(interior[0, 0])
    total, einv, weights, base, h = pl.pallas_call(
        second_kernel,
        out_shape=(sds(TILE, 2 * NS), sds(NE, NE), sds(NE, NS), sds(NI, NI), sds(NI, NS)),
        in_specs=[s, v, v, v, v],
        out_specs=(v,) * 5,
        scratch_shapes=[
            buf(TILE, NS), buf(TILE, 2 * NS), buf(TILE, 2 * NS),
            buf(64, NS), buf(64, 2 * NS), buf(64, 2 * NS),
            buf(64, NS), buf(64, 2 * NS), buf(64, 2 * NS),
            buf(8, 8, NS), buf(8, 8, 2 * NS), buf(8, 8, 2 * NS),
            buf(TILE, NS), buf(TILE, 2 * NS), buf(4, 8, 2 * NS), buf(4, 8, 2 * NS), buf(TILE, 2 * NS),
            dma((3,)), dma((3, 8)), dma((3, 16)), dma((2, 4)), dma((75,)),
        ],
        compiler_params=pltpu.CompilerParams(collective_id=0, has_side_effects=True),
    )(tile_mask[0], ainv, coupling[0, 0], prior[0], sep_map)
    result, rows = pl.pallas_call(
        third_kernel,
        out_shape=(sds(NI, NI), sds(count, NRC)),
        in_specs=[v] * 7,
        out_specs=(v, v),
        scratch_shapes=[buf(NS, NS), buf(NS, NS)],
    )(total, nat_diag[None, :], sep_map, base, h, einv, weights)
    return (result[None, None], rows[None])


def solution(mesh):
    placed = (
        P("region", "dev", None, None),
        P("region", "dev", None, None),
        P("region", "dev", None),
        P("region", "dev", None),
        P("region", None),
        P(),
    )
    return jax.shard_map(
        body,
        mesh=mesh,
        in_specs=placed,
        out_specs=(P("region", "dev", None, None), P("region", "dev", None)),
        check_vma=False,
    )
```

time: 115 us -> 80.2 us (0.70)
  Pallas kernels: 111 us -> 78.1 us
  local copies, waits for them, and re-layouts: 2.57 us -> 1.26 us
    pallas_call x2, Pallas kernels: 85.5 us -> 65.4 us  [the longest x1 55.1 us: body(): pl.pallas_call(second_kernel, out_shape=(sds(TILE, 2 * NS), sds(NE, NE),...]
    pallas_call x1, Pallas kernels: 25.5 us -> 12.7 us  [body(): pl.pallas_call(third_kernel, out_shape=(sds(NI, NI), sds(count, NRC)), in...]
    broadcast_in_dim x2 -> x0, local copies, waits for them, and re-layouts: 1.31 us -> none  [body(): own_map[:, None]]
where the time goes in v3:
time: 80.2 us; the launch traced here: 80 us
  Pallas kernels  78.1 us (97%)
  local copies, waits for them, and re-layouts  1.26 us (2%)
    pallas_call x1, Pallas kernels, body(): pl.pallas_call(second_kernel, out_shape=(sds(TILE, 2 * NS), sds(NE, NE),...  55.1 us
    pallas_call x1, Pallas kernels, body(): pl.pallas_call(third_kernel, out_shape=(sds(NI, NI), sds(count, NRC)), in...  12.7 us
    pallas_call x1, Pallas kernels, body(): pl.pallas_call(first_kernel, out_shape=sds(NI, NI), in_specs=[v], out_spe...  10.4 us

profile of v3, /device:TPU:1, one launch (start us, length us, event | category | flops | bytes accessed | tf_op | source)
XLA Modules:
  0.0 80.0 jit_solution(5226292593461989011)
XLA Ops:
  0.6 0.0 copy-start
  0.6 0.7 copy-done
  1.3 0.6 broadcast_in_dim.9.diag
  1.9 10.4 %shard_map.77.ainv = f32[384,384]{1,0:T(8,128)} custom-call(f32[384,384]{1,0:T(8,128)} %bitcast.7), custom_call_target="tpu_custom_call" | custom-call | tf_op jit(solution)/shard_map/pallas_call | solution.py:349
  12.3 55.1 %shard_map.78 = (f32[128,768]{1,0:T(8,128)}, f32[256,256]{1,0:T(8,128)}, f32[256,384]{1,0:T(8,128)}, f32[384,384]{1,0:T(8,128)}, f32[384,384]{1,0:T(8,128)}) custom-call(s32[1,5]{1,0:T(1,128)} %bitcast.9, f32[384,384]{1,0:T(8,128)} %shard_map.77.ainv, f32[384,640]{1,0:T(8,128)} %bitcast.6, f32[40,640]{1,0:T(8,128)} %bitcast.8, s32[1,384]{1,0:T(1,128)} %sep.3), custom_call_target="tpu_custom_call" | custom-call | tf_op jit(solution)/shard_map/pallas_call | solution.py:350
  67.3 12.7 %shard_map.79 = (f32[384,384]{1,0:T(8,128)}, f32[40,640]{1,0:T(8,128)}) custom-call(f32[128,768]{1,0:T(8,128)} %get-tuple-element.9.total, f32[1,384]{1,0:T(1,128)} %broadcast_in_dim.9.diag, s32[1,384]{1,0:T(1,128)} %sep.3, f32[384,384]{1,0:T(8,128)} %get-tuple-element.10.base, f32[384,384]{1,0:T(8,128)} %get-tuple-element.11.h, ...), custom_call_target="tpu_custom_call" | custom-call | tf_op jit(solution)/shard_map/pallas_call | solution.py:365
Async XLA Ops:
  0.6 0.7 copy-start

commit v4 on v3

--- a/solution.py
+++ b/solution.py
@@ -13,6 +13,7 @@
 EXACT = lax.Precision.HIGHEST
 F32 = jnp.float32
 VMEM = pltpu.VMEM
+GRANT = 24 * 1024 * 1024
 MESH = pl.DeviceIdType.MESH
 
 
@@ -170,13 +171,13 @@
 
 
 def first_kernel(interior, ainv):
-    verified_inverse(interior, ainv, 0.5, 3)
+    verified_inverse(interior, ainv, 0.5, 4)
 
 
 def second_kernel(
-    mask, ainv, coupling, prior, sep, total, einv, weights, base, h,
-    e_own, x_own, s_own, half_e, half_x, half_s, acc_e, acc_x, acc_s, rs_e, rs_x, rs_s,
-    e_all, x_all, y_all, z_all, n_all, half_sem, rs_sem, ag_sem, reg_sem, send_sem,
+    mask, ainv, coupling, prior, sep, total, weights, base, h, b_rows, e_rows,
+    e_own, x_own, s_own, half_x, half_s, acc_x, acc_s, rs_e, rs_x, rs_s, e_all, x_all, y_all, z_all, n_all,
+    einv, tiles, e_sem, half_sem, rs_sem, ag_sem, reg_sem, send_sem,
 ):
     me, region = lax.axis_index("dev"), lax.axis_index("region")
     q, core = lax.div(me, 2), lax.rem(me, 2)
@@ -252,21 +253,18 @@
     e_own[:, :TILE] = p_e[:TILE, :TILE] - dot(m_e[:, :TILE], g_e[:, :TILE], ((0,), (0,)))
     e_own[:, TILE:] = p_e[TILE:, :] - dot(m_e[:, TILE:], g_e, ((0,), (0,)))
     pl.semaphore_wait(barrier, 21)
-    halve(0, e_own, half_e)
+    for other in others:
+        send(e_own.at[rows_of(other), :], rs_e.at[me], e_sem.at[me], dev=other)
 
     m_s = jnp.concatenate([coupling[:, TILE * t : TILE * (t + 1)] * mask[0, t].astype(F32) for t in range(2, 5)], axis=1)
     m_s = select_right(m_s, perm, ((1,), (1,)))
-    scatter(0, e_own, half_e, acc_e, rs_e)
     g_s = fast(ainv[...], m_s)
     p_s = select_right(prior[:, NE:], perm, ((1,), (1,)))
     p_x = select_left(place_e, p_s)
     x_term = dot(m_e, g_s, ((0,), (0,)))
     x_own[:, :NS] = p_x[:TILE] - x_term[:TILE]
     x_own[:, NS:] = p_x[TILE:] - x_term[TILE:]
-    halve(1, x_own, half_x)
-    e_all[rows_of(me), :] = gathered(0, acc_e, rs_e)
-    spread(0, e_all)
-    scatter(1, x_own, half_x, acc_x, rs_x)
+    halve(0, x_own, half_x)
     at = lax.broadcasted_iota(jnp.int32, (NS, count), 1) + (me * count - NE)
     local = (lax.broadcasted_iota(jnp.int32, (NS, count), 0) == at).astype(jnp.bfloat16)
     place_s = lax.dot_general(perm, local, (((1,), (0,)), ((), ())), preferred_element_type=F32).astype(jnp.bfloat16)
@@ -274,16 +272,39 @@
     s_own[:, :TILE] = p_s[:TILE, :TILE] - dot(m_s[:, :TILE], g_s[:, :TILE], ((0,), (0,)))
     s_own[:, TILE : 3 * TILE] = p_s[TILE:NE, :NE] - dot(m_s[:, TILE:NE], g_s[:, :NE], ((0,), (0,)))
     s_own[:, 3 * TILE :] = p_s[NE:, :] - dot(m_s[:, NE:], g_s, ((0,), (0,)))
-    halve(2, s_own, half_s)
-    x_all[rows_of(me), :] = gathered(1, acc_x, rs_x)
+    halve(1, s_own, half_s)
+
+    value = e_own[rows_of(me), :]
+    for other in others:
+        arrived(rs_e.at[other], e_sem.at[other])
+        value = value + rs_e[other]
+    e_all[rows_of(me), :] = value
+    spread(0, e_all)
+    scatter(0, x_own, half_x, acc_x, rs_x)
+    x_all[rows_of(me), :] = gathered(0, acc_x, rs_x)
     spread(1, x_all)
-    scatter(2, s_own, half_s, acc_s, rs_s)
+    scatter(1, s_own, half_s, acc_s, rs_s)
 
     complete(0, e_all)
-    einv[:TILE, :TILE] = e_all[:, :TILE]
-    einv[TILE:, :] = e_all[:, TILE:]
-    einv[:TILE, TILE:] = e_all[:, TILE:NE].T
-    invert(einv, NE // TILE)
+    tiles[0] = e_all[:, :TILE]
+
+    def pivot(k, _):
+        block = tiles[k]
+        tiles[k] = jnp.concatenate(inverse128([block[8 * i : 8 * i + 8, :] for i in range(TILE // 8)]), axis=0)
+
+        @pl.when(k == 0)
+        def _():
+            tiles[2] = dot(e_all[:, TILE:NE], tiles[0])
+            tiles[1] = e_all[:, NE:] - dot(tiles[2], e_all[:, TILE:NE], ((1,), (1,)))
+
+        return 0
+
+    lax.fori_loop(0, 2, pivot, 0)
+    lower = dot(tiles[1], tiles[2])
+    einv[:TILE, :TILE] = tiles[0] + dot(tiles[2], lower, ((0,), (0,)))
+    einv[TILE:, :TILE] = -lower
+    einv[:TILE, TILE:] = -lower.T
+    einv[TILE:, TILE:] = tiles[1]
     complete(1, x_all)
     cross = jnp.concatenate([x_all[:, :NS], x_all[:, NS:]], axis=0)
     w = dot(einv[...], cross)
@@ -293,7 +314,7 @@
     part = dot(select_left(pick, cross, ((1,), (1,))), w)
     part = jnp.concatenate([part[:8, :TILE], part[8:16, :NE], part[16:, :]], axis=1)
 
-    y_all[y] = gathered(2, acc_s, rs_s) - part
+    y_all[y] = gathered(1, acc_s, rs_s) - part
     for other in y_peers:
         send(y_all.at[y], y_all.at[y], reg_sem.at[0, y], region=other * 4 + z)
     h[...] = g_s - dot(g_e, w)
@@ -307,14 +328,19 @@
         arrived(z_all.at[other], reg_sem.at[1, other])
     n_all[rows_of(me), :] = (z_all[0] + z_all[1]) + (z_all[2] + z_all[3])
     spread(2, n_all)
+    at = lambda n: lax.broadcasted_iota(jnp.int32, (count, n), 0) + me * count
+    pick_e = (lax.broadcasted_iota(jnp.int32, (count, NE), 1) == at(NE)).astype(jnp.bfloat16)
+    pick_s = (lax.broadcasted_iota(jnp.int32, (count, NS), 1) + NE == at(NS)).astype(jnp.bfloat16)
+    pick_s = lax.dot_general(pick_s, perm, (((1,), (1,)), ((), ())), preferred_element_type=F32)
+    b_rows[...] = pick_s - select_left(pick_e, w)
+    e_rows[...] = select_left(pick_e, einv[...])
     complete(2, n_all)
     total[...] = n_all[...]
     for copy in sent:
         copy.wait_send()
 
 
-def third_kernel(total, diag, sep, base, h, einv, weights, out, rows, normal, inverse):
-    me = lax.axis_index("dev")
+def third_kernel(total, diag, sep, base, h, weights, b_rows, e_rows, out, rows, normal, inverse):
     t0, t1, t2 = total[:, :TILE], total[:, TILE : 3 * TILE], total[:, 3 * TILE :]
     normal[:TILE, :TILE] = t0
     normal[TILE:NE, :NE] = t1
@@ -323,20 +349,14 @@
     normal[:TILE, NE:] = t2[:, :TILE].T
     normal[TILE:NE, NE:] = t2[:, TILE:NE].T
     i0, i1 = (lax.broadcasted_iota(jnp.int32, (NS, NS), d) for d in (0, 1))
-    normal[...] = normal[...] + jnp.where(i0 == i1, diag[...], 0.0)
-    verified_inverse(normal, inverse, 0.25, 2)
+    normal[...] = normal[...] + jnp.where(i0 == i1, diag[...].reshape(1, NS), 0.0)
+    verified_inverse(normal, inverse, 0.25, 3)
     x = inverse[...]
     w = weights[...]
     out[...] = base[...] + fast(fast(h[...], x), h[...], ((1,), (1,)))
-    count = rows.shape[0]
-    perm = national(sep[...])
-    at = lambda n: lax.broadcasted_iota(jnp.int32, (count, n), 0) + me * count
-    pick_e = (lax.broadcasted_iota(jnp.int32, (count, NE), 1) == at(NE)).astype(jnp.bfloat16)
-    pick_s = (lax.broadcasted_iota(jnp.int32, (count, NS), 1) + NE == at(NS)).astype(jnp.bfloat16)
-    pick_s = lax.dot_general(pick_s, perm, (((1,), (1,)), ((), ())), preferred_element_type=F32)
-    t = dot(pick_s - select_left(pick_e, w), x)
-    rows[:, :NE] = select_left(pick_e, einv[...]) - dot(t, w, ((1,), (1,)))
-    rows[:, NE:] = select_right(t, perm)
+    t = fast(b_rows[...], x)
+    rows[:, :NE] = e_rows[...] - fast(t, w, ((1,), (1,)))
+    rows[:, NE:] = select_right(t, national(sep[...]))
 
 
 def body(interior, coupling, tile_mask, prior, sep_map, nat_diag):
@@ -346,29 +366,36 @@
     s = pl.BlockSpec(memory_space=pltpu.SMEM)
     dma = pltpu.SemaphoreType.DMA
     buf = lambda *shape: VMEM(shape, F32)
-    ainv = pl.pallas_call(first_kernel, out_shape=sds(NI, NI), in_specs=[v], out_specs=v)(interior[0, 0])
-    total, einv, weights, base, h = pl.pallas_call(
+    ainv = pl.pallas_call(
+        first_kernel,
+        out_shape=sds(NI, NI),
+        in_specs=[v],
+        out_specs=v,
+        compiler_params=pltpu.CompilerParams(vmem_limit_bytes=GRANT),
+    )(interior[0, 0])
+    total, weights, base, h, b_rows, e_rows = pl.pallas_call(
         second_kernel,
-        out_shape=(sds(TILE, 2 * NS), sds(NE, NE), sds(NE, NS), sds(NI, NI), sds(NI, NS)),
+        out_shape=(sds(TILE, 2 * NS), sds(NE, NS), sds(NI, NI), sds(NI, NS), sds(count, NS), sds(count, NE)),
         in_specs=[s, v, v, v, v],
-        out_specs=(v,) * 5,
+        out_specs=(v,) * 6,
         scratch_shapes=[
             buf(TILE, NS), buf(TILE, 2 * NS), buf(TILE, 2 * NS),
-            buf(64, NS), buf(64, 2 * NS), buf(64, 2 * NS),
-            buf(64, NS), buf(64, 2 * NS), buf(64, 2 * NS),
-            buf(8, 8, NS), buf(8, 8, 2 * NS), buf(8, 8, 2 * NS),
+            buf(64, 2 * NS), buf(64, 2 * NS), buf(64, 2 * NS), buf(64, 2 * NS),
+            buf(16, 8, NS), buf(8, 8, 2 * NS), buf(8, 8, 2 * NS),
             buf(TILE, NS), buf(TILE, 2 * NS), buf(4, 8, 2 * NS), buf(4, 8, 2 * NS), buf(TILE, 2 * NS),
-            dma((3,)), dma((3, 8)), dma((3, 16)), dma((2, 4)), dma((75,)),
+            buf(NE, NE), buf(3, TILE, TILE),
+            dma((16,)), dma((2,)), dma((2, 8)), dma((3, 16)), dma((2, 4)), dma((82,)),
         ],
-        compiler_params=pltpu.CompilerParams(collective_id=0, has_side_effects=True),
+        compiler_params=pltpu.CompilerParams(collective_id=0, has_side_effects=True, vmem_limit_bytes=GRANT),
     )(tile_mask[0], ainv, coupling[0, 0], prior[0], sep_map)
     result, rows = pl.pallas_call(
         third_kernel,
         out_shape=(sds(NI, NI), sds(count, NRC)),
-        in_specs=[v] * 7,
+        in_specs=[v] * 8,
         out_specs=(v, v),
         scratch_shapes=[buf(NS, NS), buf(NS, NS)],
-    )(total, nat_diag[None, :], sep_map, base, h, einv, weights)
+        compiler_params=pltpu.CompilerParams(vmem_limit_bytes=GRANT),
+    )(total, nat_diag, sep_map, base, h, weights, b_rows, e_rows)
     return (result[None, None], rows[None])
 
 

time: 80.2 us -> 69.6 us (0.87)
  Pallas kernels: 78.1 us -> 66.9 us
    pallas_call x1, Pallas kernels: 12.7 us -> 8.65 us  [body(): pl.pallas_call(third_kernel, out_shape=(sds(NI, NI), sds(count, NRC)), in...]
    pallas_call x1, Pallas kernels: 55.1 us -> 51.5 us  [body(): pl.pallas_call(second_kernel, out_shape=(sds(TILE, 2 * NS), sds(NE, NS),...]
    pallas_call x1, Pallas kernels: 10.4 us -> 6.81 us  [body(): pl.pallas_call(first_kernel, out_shape=sds(NI, NI), in_specs=[v], out_spe...]
    unnamed x2 -> x12, local copies, waits for them, and re-layouts: 0.67 us -> 1.83 us
where the time goes in v4:
time: 69.6 us; the launch traced here: 69.5 us
  Pallas kernels  66.9 us (96%)
  local copies, waits for them, and re-layouts  1.83 us (3%)
  between operations  0.71 us (1%)
    pallas_call x1, Pallas kernels, body(): pl.pallas_call(second_kernel, out_shape=(sds(TILE, 2 * NS), sds(NE, NS),...  51.5 us
    pallas_call x1, Pallas kernels, body(): pl.pallas_call(third_kernel, out_shape=(sds(NI, NI), sds(count, NRC)), in...  8.65 us
    pallas_call x1, Pallas kernels, body(): pl.pallas_call(first_kernel, out_shape=sds(NI, NI), in_specs=[v], out_spe...  6.81 us
    unnamed x12, local copies, waits for them, and re-layouts  1.83 us

profile of v4, /device:TPU:1, one launch (start us, length us, event | category | flops | bytes accessed | tf_op | source)
XLA Modules:
  0.0 69.5 jit_solution(6351016626140572958)
XLA Ops:
  0.6 0.0 copy-start
  0.6 0.0 copy-start.1
  0.7 1.1 %copy-done.1 = f32[1,1,384,384]{3,2,1,0:T(8,128)S(1)} copy-done((f32[1,1,384,384]{3,2,1,0:T(8,128)S(1)}, f32[1,1,384,384]{3,2,1,0:T(8,128)}, u32[]{:S(2)}) %copy-start.1) | copy-done | bytes 589848
  1.8 0.0 copy-start.2
  1.8 0.0 copy-start.3
  1.8 0.0 copy-start.5
  1.8 6.8 %shard_map.77.ainv = f32[384,384]{1,0:T(8,128)S(1)} custom-call(f32[384,384]{1,0:T(8,128)S(1)} %bitcast.7), custom_call_target="tpu_custom_call" | custom-call | tf_op jit(solution)/shard_map/pallas_call | solution.py:369
  8.6 0.0 copy-done
  8.6 0.0 copy-done.2
  8.6 0.0 copy-done.3
  8.6 0.0 copy-done.5
  8.6 51.5 %shard_map.78 = (f32[128,768]{1,0:T(8,128)S(1)}, f32[256,384]{1,0:T(8,128)S(1)}, f32[384,384]{1,0:T(8,128)S(1)}, f32[384,384]{1,0:T(8,128)S(1)}, f32[40,384]{1,0:T(8,128)S(1)}, /*index=5*/f32[40,256]{1,0:T(8,128)S(1)}) custom-call(s32[1,5]{1,0:T(1,128)S(1)} %bitcast.9, f32[384,384]{1,0:T(8,128)S(1)} %shard_map.77.ainv, f32[384,640]{1,0:T(8,128)S(1)} %bitcast.6, ...), custom_call_target="tpu_custom_call" | custom-call | tf_op jit(solution)/shard_map/pallas_call | solution.py:376
  60.1 0.0 copy-start.4
  60.1 0.7 copy-done.4
  60.8 8.6 %shard_map.79 = (f32[384,384]{1,0:T(8,128)}, f32[40,640]{1,0:T(8,128)}) custom-call(f32[128,768]{1,0:T(8,128)S(1)} %get-tuple-element.10.total, f32[384]{0:T(512)S(1)} %copy-done.4, s32[1,384]{1,0:T(1,128)S(1)} %copy-done.3, f32[384,384]{1,0:T(8,128)S(1)} %get-tuple-element.11.base, f32[384,384]{1,0:T(8,128)S(1)} %get-tuple-element.12.h, ...), custom_call_target="tpu_custom_call" | custom-call | tf_op jit(solution)/shard_map/pallas_call | solution.py:391
Async XLA Ops:
  0.6 8.0 %copy-start = (f32[1,1,384,640]{3,2,1,0:T(8,128)S(1)}, f32[1,1,384,640]{3,2,1,0:T(8,128)}, u32[]{:S(2)}) copy-start(f32[1,1,384,640]{3,2,1,0:T(8,128)} %param.7) | copy-start | bytes 2949124
  0.6 1.1 %copy-start.1 = (f32[1,1,384,384]{3,2,1,0:T(8,128)S(1)}, f32[1,1,384,384]{3,2,1,0:T(8,128)}, u32[]{:S(2)}) copy-start(f32[1,1,384,384]{3,2,1,0:T(8,128)} %param.6) | copy-start | bytes 1769476
  1.8 6.8 %copy-start.2 = (f32[1,40,640]{2,1,0:T(8,128)S(1)}, f32[1,40,640]{2,1,0:T(8,128)}, u32[]{:S(2)}) copy-start(f32[1,40,640]{2,1,0:T(8,128)} %param.9) | copy-start | bytes 307204
  1.8 6.8 %copy-start.3 = (s32[1,384]{1,0:T(1,128)S(1)}, s32[1,384]{1,0:T(1,128)}, u32[]{:S(2)}) copy-start(s32[1,384]{1,0:T(1,128)} %sep.3) | copy-start | bytes 4612
  1.8 6.8 %copy-start.5 = (s32[1,1,5]{2,1,0:T(1,128)S(1)}, s32[1,1,5]{2,1,0:T(1,128)}, u32[]{:S(2)}) copy-start(s32[1,1,5]{2,1,0:T(1,128)} %param.8) | copy-start | bytes 64
  60.1 0.7 copy-start.4

commit v5 on v4

--- a/solution.py
+++ b/solution.py
@@ -265,6 +265,13 @@
     x_own[:, :NS] = p_x[:TILE] - x_term[:TILE]
     x_own[:, NS:] = p_x[TILE:] - x_term[TILE:]
     halve(0, x_own, half_x)
+    value = e_own[rows_of(me), :]
+    for other in others:
+        arrived(rs_e.at[other], e_sem.at[other])
+        value = value + rs_e[other]
+    e_all[rows_of(me), :] = value
+    spread(0, e_all)
+    scatter(0, x_own, half_x, acc_x, rs_x)
     at = lax.broadcasted_iota(jnp.int32, (NS, count), 1) + (me * count - NE)
     local = (lax.broadcasted_iota(jnp.int32, (NS, count), 0) == at).astype(jnp.bfloat16)
     place_s = lax.dot_general(perm, local, (((1,), (0,)), ((), ())), preferred_element_type=F32).astype(jnp.bfloat16)
@@ -274,13 +281,6 @@
     s_own[:, 3 * TILE :] = p_s[NE:, :] - dot(m_s[:, NE:], g_s, ((0,), (0,)))
     halve(1, s_own, half_s)
 
-    value = e_own[rows_of(me), :]
-    for other in others:
-        arrived(rs_e.at[other], e_sem.at[other])
-        value = value + rs_e[other]
-    e_all[rows_of(me), :] = value
-    spread(0, e_all)
-    scatter(0, x_own, half_x, acc_x, rs_x)
     x_all[rows_of(me), :] = gathered(0, acc_x, rs_x)
     spread(1, x_all)
     scatter(1, s_own, half_s, acc_s, rs_s)
@@ -307,16 +307,16 @@
     einv[TILE:, TILE:] = tiles[1]
     complete(1, x_all)
     cross = jnp.concatenate([x_all[:, :NS], x_all[:, NS:]], axis=0)
-    w = dot(einv[...], cross)
-    weights[...] = w
     i0, i1 = (lax.broadcasted_iota(jnp.int32, (24, NS), d) for d in (0, 1))
     pick = (i1 == lax.div(i0, 8) * TILE + lax.rem(i0, 8) + core * 64 + q * 8).astype(jnp.bfloat16)
-    part = dot(select_left(pick, cross, ((1,), (1,))), w)
+    part = dot(dot(select_left(pick, cross, ((1,), (1,))), einv[...]), cross)
     part = jnp.concatenate([part[:8, :TILE], part[8:16, :NE], part[16:, :]], axis=1)
 
     y_all[y] = gathered(1, acc_s, rs_s) - part
     for other in y_peers:
         send(y_all.at[y], y_all.at[y], reg_sem.at[0, y], region=other * 4 + z)
+    w = dot(einv[...], cross)
+    weights[...] = w
     h[...] = g_s - dot(g_e, w)
     for other in y_peers:
         arrived(y_all.at[other], reg_sem.at[0, other])

time: 69.6 us -> 69.4 us (level)
  no operation moved by 1% of the time
where the time goes in v5:
time: 69.4 us; the launch traced here: 69.2 us
  Pallas kernels  66.7 us (96%)
  local copies, waits for them, and re-layouts  1.83 us (3%)
  between operations  0.71 us (1%)
    pallas_call x1, Pallas kernels, body(): pl.pallas_call(second_kernel, out_shape=(sds(TILE, 2 * NS), sds(NE, NS),...  51.1 us
    pallas_call x1, Pallas kernels, body(): pl.pallas_call(third_kernel, out_shape=(sds(NI, NI), sds(count, NRC)), in...  8.84 us
    pallas_call x1, Pallas kernels, body(): pl.pallas_call(first_kernel, out_shape=sds(NI, NI), in_specs=[v], out_spe...  6.81 us
    unnamed x12, local copies, waits for them, and re-layouts  1.83 us

profile of v5, /device:TPU:1, one launch (start us, length us, event | category | flops | bytes accessed | tf_op | source)
XLA Modules:
  0.0 69.2 jit_solution(17234312092438687014)
XLA Ops:
  0.6 0.0 copy-start
  0.6 0.0 copy-start.1
  0.7 1.1 %copy-done.1 = f32[1,1,384,384]{3,2,1,0:T(8,128)S(1)} copy-done((f32[1,1,384,384]{3,2,1,0:T(8,128)S(1)}, f32[1,1,384,384]{3,2,1,0:T(8,128)}, u32[]{:S(2)}) %copy-start.1) | copy-done | bytes 589848
  1.8 0.0 copy-start.2
  1.8 0.0 copy-start.3
  1.8 0.0 copy-start.5
  1.8 6.8 %shard_map.77.ainv = f32[384,384]{1,0:T(8,128)S(1)} custom-call(f32[384,384]{1,0:T(8,128)S(1)} %bitcast.7), custom_call_target="tpu_custom_call" | custom-call | tf_op jit(solution)/shard_map/pallas_call | solution.py:369
  8.6 0.0 copy-done
  8.6 0.0 copy-done.2
  8.6 0.0 copy-done.3
  8.6 0.0 copy-done.5
  8.6 51.1 %shard_map.78 = (f32[128,768]{1,0:T(8,128)S(1)}, f32[256,384]{1,0:T(8,128)S(1)}, f32[384,384]{1,0:T(8,128)S(1)}, f32[384,384]{1,0:T(8,128)S(1)}, f32[40,384]{1,0:T(8,128)S(1)}, /*index=5*/f32[40,256]{1,0:T(8,128)S(1)}) custom-call(s32[1,5]{1,0:T(1,128)S(1)} %bitcast.9, f32[384,384]{1,0:T(8,128)S(1)} %shard_map.77.ainv, f32[384,640]{1,0:T(8,128)S(1)} %bitcast.6, ...), custom_call_target="tpu_custom_call" | custom-call | tf_op jit(solution)/shard_map/pallas_call | solution.py:376
  59.7 0.0 copy-start.4
  59.7 0.7 copy-done.4
  60.4 8.8 %shard_map.79 = (f32[384,384]{1,0:T(8,128)}, f32[40,640]{1,0:T(8,128)}) custom-call(f32[128,768]{1,0:T(8,128)S(1)} %get-tuple-element.10.total, f32[384]{0:T(512)S(1)} %copy-done.4, s32[1,384]{1,0:T(1,128)S(1)} %copy-done.3, f32[384,384]{1,0:T(8,128)S(1)} %get-tuple-element.11.base, f32[384,384]{1,0:T(8,128)S(1)} %get-tuple-element.12.h, ...), custom_call_target="tpu_custom_call" | custom-call | tf_op jit(solution)/shard_map/pallas_call | solution.py:391
Async XLA Ops:
  0.6 8.0 %copy-start = (f32[1,1,384,640]{3,2,1,0:T(8,128)S(1)}, f32[1,1,384,640]{3,2,1,0:T(8,128)}, u32[]{:S(2)}) copy-start(f32[1,1,384,640]{3,2,1,0:T(8,128)} %param.7) | copy-start | bytes 2949124
  0.6 1.1 %copy-start.1 = (f32[1,1,384,384]{3,2,1,0:T(8,128)S(1)}, f32[1,1,384,384]{3,2,1,0:T(8,128)}, u32[]{:S(2)}) copy-start(f32[1,1,384,384]{3,2,1,0:T(8,128)} %param.6) | copy-start | bytes 1769476
  1.8 6.8 %copy-start.2 = (f32[1,40,640]{2,1,0:T(8,128)S(1)}, f32[1,40,640]{2,1,0:T(8,128)}, u32[]{:S(2)}) copy-start(f32[1,40,640]{2,1,0:T(8,128)} %param.9) | copy-start | bytes 307204
  1.8 6.8 %copy-start.3 = (s32[1,384]{1,0:T(1,128)S(1)}, s32[1,384]{1,0:T(1,128)}, u32[]{:S(2)}) copy-start(s32[1,384]{1,0:T(1,128)} %sep.3) | copy-start | bytes 4612
  1.8 6.8 %copy-start.5 = (s32[1,1,5]{2,1,0:T(1,128)S(1)}, s32[1,1,5]{2,1,0:T(1,128)}, u32[]{:S(2)}) copy-start(s32[1,1,5]{2,1,0:T(1,128)} %param.8) | copy-start | bytes 64
  59.7 0.7 copy-start.4

commit v6 on v5

--- a/solution.py
+++ b/solution.py
@@ -175,7 +175,7 @@
 
 
 def second_kernel(
-    mask, ainv, coupling, prior, sep, total, weights, base, h, b_rows, e_rows,
+    mask, ainv, coupling, prior, sep, diag, normal, weights, base, h, b_rows, e_rows,
     e_own, x_own, s_own, half_x, half_s, acc_x, acc_s, rs_e, rs_x, rs_s, e_all, x_all, y_all, z_all, n_all,
     einv, tiles, e_sem, half_sem, rs_sem, ag_sem, reg_sem, send_sem,
 ):
@@ -242,6 +242,18 @@
     def complete(kind, full):
         for other in others:
             arrived(full.at[rows_of(other), :], ag_sem.at[kind, other])
+
+    def near(kind, full):
+        for dev in [other * 2 + core for other in same_core] + [partner]:
+            send(full.at[rows_of(me), :], full.at[rows_of(me), :], ag_sem.at[kind, me], dev=dev)
+
+    def far(kind, full):
+        for other in same_core:
+            dev = other * 2 + core
+            arrived(full.at[rows_of(dev), :], ag_sem.at[kind, dev])
+            send(full.at[rows_of(dev), :], full.at[rows_of(dev), :], ag_sem.at[kind, dev], dev=partner)
+        for dev in [partner] + [other * 2 + 1 - core for other in same_core]:
+            arrived(full.at[rows_of(dev), :], ag_sem.at[kind, dev])
 
     count = prior.shape[0]
     perm = national(sep[...])
@@ -327,29 +339,28 @@
     for other in z_peers:
         arrived(z_all.at[other], reg_sem.at[1, other])
     n_all[rows_of(me), :] = (z_all[0] + z_all[1]) + (z_all[2] + z_all[3])
-    spread(2, n_all)
+    near(2, n_all)
     at = lambda n: lax.broadcasted_iota(jnp.int32, (count, n), 0) + me * count
     pick_e = (lax.broadcasted_iota(jnp.int32, (count, NE), 1) == at(NE)).astype(jnp.bfloat16)
     pick_s = (lax.broadcasted_iota(jnp.int32, (count, NS), 1) + NE == at(NS)).astype(jnp.bfloat16)
     pick_s = lax.dot_general(pick_s, perm, (((1,), (1,)), ((), ())), preferred_element_type=F32)
     b_rows[...] = pick_s - select_left(pick_e, w)
     e_rows[...] = select_left(pick_e, einv[...])
-    complete(2, n_all)
-    total[...] = n_all[...]
-    for copy in sent:
-        copy.wait_send()
-
-
-def third_kernel(total, diag, sep, base, h, weights, b_rows, e_rows, out, rows, normal, inverse):
-    t0, t1, t2 = total[:, :TILE], total[:, TILE : 3 * TILE], total[:, 3 * TILE :]
+    far(2, n_all)
+    i0, i1 = (lax.broadcasted_iota(jnp.int32, (NS, NS), d) for d in (0, 1))
+    t0, t1, t2 = n_all[:, :TILE], n_all[:, TILE : 3 * TILE], n_all[:, 3 * TILE :]
     normal[:TILE, :TILE] = t0
     normal[TILE:NE, :NE] = t1
     normal[NE:, :] = t2
     normal[:TILE, TILE:NE] = t1[:, :TILE].T
     normal[:TILE, NE:] = t2[:, :TILE].T
     normal[TILE:NE, NE:] = t2[:, TILE:NE].T
-    i0, i1 = (lax.broadcasted_iota(jnp.int32, (NS, NS), d) for d in (0, 1))
     normal[...] = normal[...] + jnp.where(i0 == i1, diag[...].reshape(1, NS), 0.0)
+    for copy in sent:
+        copy.wait_send()
+
+
+def third_kernel(normal, sep, base, h, weights, b_rows, e_rows, out, rows, inverse):
     verified_inverse(normal, inverse, 0.25, 3)
     x = inverse[...]
     w = weights[...]
@@ -373,10 +384,10 @@
         out_specs=v,
         compiler_params=pltpu.CompilerParams(vmem_limit_bytes=GRANT),
     )(interior[0, 0])
-    total, weights, base, h, b_rows, e_rows = pl.pallas_call(
+    normal, weights, base, h, b_rows, e_rows = pl.pallas_call(
         second_kernel,
-        out_shape=(sds(TILE, 2 * NS), sds(NE, NS), sds(NI, NI), sds(NI, NS), sds(count, NS), sds(count, NE)),
-        in_specs=[s, v, v, v, v],
+        out_shape=(sds(NS, NS), sds(NE, NS), sds(NI, NI), sds(NI, NS), sds(count, NS), sds(count, NE)),
+        in_specs=[s, v, v, v, v, v],
         out_specs=(v,) * 6,
         scratch_shapes=[
             buf(TILE, NS), buf(TILE, 2 * NS), buf(TILE, 2 * NS),
@@ -387,15 +398,15 @@
             dma((16,)), dma((2,)), dma((2, 8)), dma((3, 16)), dma((2, 4)), dma((82,)),
         ],
         compiler_params=pltpu.CompilerParams(collective_id=0, has_side_effects=True, vmem_limit_bytes=GRANT),
-    )(tile_mask[0], ainv, coupling[0, 0], prior[0], sep_map)
+    )(tile_mask[0], ainv, coupling[0, 0], prior[0], sep_map, nat_diag)
     result, rows = pl.pallas_call(
         third_kernel,
         out_shape=(sds(NI, NI), sds(count, NRC)),
-        in_specs=[v] * 8,
+        in_specs=[v] * 7,
         out_specs=(v, v),
-        scratch_shapes=[buf(NS, NS), buf(NS, NS)],
+        scratch_shapes=[buf(NS, NS)],
         compiler_params=pltpu.CompilerParams(vmem_limit_bytes=GRANT),
-    )(total, nat_diag, sep_map, base, h, weights, b_rows, e_rows)
+    )(normal, sep_map, base, h, weights, b_rows, e_rows)
     return (result[None, None], rows[None])
 
 

time: 69.4 us -> 69.4 us (level)
  Pallas kernels: 66.7 us -> 67.4 us
    pallas_call x1, Pallas kernels: 51.1 us -> 51.8 us  [body(): pl.pallas_call(second_kernel, out_shape=(sds(NS, NS), sds(NE, NS), sds(NI...]
where the time goes in v6:
time: 69.4 us; the launch traced here: 69.3 us
  Pallas kernels  67.4 us (97%)
  local copies, waits for them, and re-layouts  1.16 us (2%)
  between operations  0.71 us (1%)
    pallas_call x1, Pallas kernels, body(): pl.pallas_call(second_kernel, out_shape=(sds(NS, NS), sds(NE, NS), sds(NI...  51.8 us
    pallas_call x1, Pallas kernels, body(): pl.pallas_call(third_kernel, out_shape=(sds(NI, NI), sds(count, NRC)), in...  8.78 us
    pallas_call x1, Pallas kernels, body(): pl.pallas_call(first_kernel, out_shape=sds(NI, NI), in_specs=[v], out_spe...  6.81 us

profile of v6, /device:TPU:1, one launch (start us, length us, event | category | flops | bytes accessed | tf_op | source)
XLA Modules:
  0.0 69.3 jit_solution(17394160288376618810)
XLA Ops:
  0.6 0.0 copy-start
  0.6 0.0 copy-start.1
  0.7 1.1 %copy-done.1 = f32[1,1,384,384]{3,2,1,0:T(8,128)S(1)} copy-done((f32[1,1,384,384]{3,2,1,0:T(8,128)S(1)}, f32[1,1,384,384]{3,2,1,0:T(8,128)}, u32[]{:S(2)}) %copy-start.1) | copy-done | bytes 589848
  1.8 0.0 copy-start.2
  1.8 0.0 copy-start.3
  1.8 0.0 copy-start.4
  1.8 0.0 copy-start.5
  1.8 6.8 %shard_map.77.ainv = f32[384,384]{1,0:T(8,128)S(1)} custom-call(f32[384,384]{1,0:T(8,128)S(1)} %bitcast.7), custom_call_target="tpu_custom_call" | custom-call | tf_op jit(solution)/shard_map/pallas_call | solution.py:380
  8.6 0.0 copy-done
  8.6 0.0 copy-done.2
  8.6 0.0 copy-done.3
  8.7 0.0 copy-done.4
  8.7 0.0 copy-done.5
  8.7 51.8 %shard_map.78 = (f32[384,384]{1,0:T(8,128)S(1)}, f32[256,384]{1,0:T(8,128)S(1)}, f32[384,384]{1,0:T(8,128)S(1)}, f32[384,384]{1,0:T(8,128)S(1)}, f32[40,384]{1,0:T(8,128)S(1)}, /*index=5*/f32[40,256]{1,0:T(8,128)S(1)}) custom-call(s32[1,5]{1,0:T(1,128)S(1)} %bitcast.9, f32[384,384]{1,0:T(8,128)S(1)} %shard_map.77.ainv, f32[384,640]{1,0:T(8,128)S(1)} %bitcast.6, ...), custom_call_target="tpu_custom_call" | custom-call | tf_op jit(solution)/shard_map/pallas_call | solution.py:387
  60.5 8.8 %shard_map.79 = (f32[384,384]{1,0:T(8,128)}, f32[40,640]{1,0:T(8,128)}) custom-call(f32[384,384]{1,0:T(8,128)S(1)} %get-tuple-element.10.normal, s32[1,384]{1,0:T(1,128)S(1)} %copy-done.3, f32[384,384]{1,0:T(8,128)S(1)} %get-tuple-element.11.base, f32[384,384]{1,0:T(8,128)S(1)} %get-tuple-element.12.h, f32[256,384]{1,0:T(8,128)S(1)} %get-tuple-element.13.weights, ...), custom_call_target="tpu_custom_call" | custom-call | tf_op jit(solution)/shard_map/pallas_call | solution.py:402
Async XLA Ops:
  0.6 8.0 %copy-start = (f32[1,1,384,640]{3,2,1,0:T(8,128)S(1)}, f32[1,1,384,640]{3,2,1,0:T(8,128)}, u32[]{:S(2)}) copy-start(f32[1,1,384,640]{3,2,1,0:T(8,128)} %param.7) | copy-start | bytes 2949124
  0.6 1.1 %copy-start.1 = (f32[1,1,384,384]{3,2,1,0:T(8,128)S(1)}, f32[1,1,384,384]{3,2,1,0:T(8,128)}, u32[]{:S(2)}) copy-start(f32[1,1,384,384]{3,2,1,0:T(8,128)} %param.6) | copy-start | bytes 1769476
  1.8 6.8 %copy-start.2 = (f32[1,40,640]{2,1,0:T(8,128)S(1)}, f32[1,40,640]{2,1,0:T(8,128)}, u32[]{:S(2)}) copy-start(f32[1,40,640]{2,1,0:T(8,128)} %param.9) | copy-start | bytes 307204
  1.8 6.9 %copy-start.3 = (s32[1,384]{1,0:T(1,128)S(1)}, s32[1,384]{1,0:T(1,128)}, u32[]{:S(2)}) copy-start(s32[1,384]{1,0:T(1,128)} %sep.3) | copy-start | bytes 4612
  1.8 6.9 %copy-start.4 = (f32[384]{0:T(512)S(1)}, f32[384]{0:T(512)}, u32[]{:S(2)}) copy-start(f32[384]{0:T(512)} %diag.1) | copy-start | bytes 4612
  1.8 6.9 %copy-start.5 = (s32[1,1,5]{2,1,0:T(1,128)S(1)}, s32[1,1,5]{2,1,0:T(1,128)}, u32[]{:S(2)}) copy-start(s32[1,1,5]{2,1,0:T(1,128)} %param.8) | copy-start | bytes 64

commit v7 on v6

--- a/solution.py
+++ b/solution.py
@@ -141,26 +141,27 @@
     for _ in range(steps):
         scale = 2.0 / (2.0 - rho * rho)
         now = x[...]
-        x[...] = (now * 2.0 - rough(now, rough(full, now))) * scale
+        x[...] = (now + rough(now, eye - rough(full, now))) * scale
         rho = rho * rho / (2.0 - rho * rho)
 
-    def more(state):
-        count, size = state
-        return jnp.logical_and(count < 12, jnp.logical_not(size <= 1e-3))
-
-    def step(state):
-        count, _ = state
-        now = x[...]
-        r = eye - fast(a[...], now)
-        x[...] = now + rough(now, r)
-        return count + 1, jnp.sum(r * r)
-
-    lax.while_loop(more, step, (jnp.int32(0), jnp.float32(1.0)))
-    now = x[...]
-    r = eye - dot(a[...], now)
-    x[...] = now + rough(now, r)
-
-    @pl.when(jnp.logical_not(jnp.sum(r * r) <= 1e-6))
+    def refine(multiply, limit, most):
+        def more(state):
+            count, size = state
+            return jnp.logical_and(count < most, jnp.logical_not(size <= limit))
+
+        def step(state):
+            count, _ = state
+            now = x[...]
+            r = eye - multiply(a[...], now)
+            x[...] = now + rough(now, r)
+            return count + 1, jnp.sum(r * r)
+
+        return lax.while_loop(more, step, (jnp.int32(0), jnp.float32(1.0)))[1]
+
+    refine(fast, 1e-2, 12)
+    size = refine(dot, 4e-6, 4)
+
+    @pl.when(jnp.logical_not(size <= 4e-6))
     def _():
         x[...] = a[...]
         invert(x, n // TILE)
@@ -361,7 +362,7 @@
 
 
 def third_kernel(normal, sep, base, h, weights, b_rows, e_rows, out, rows, inverse):
-    verified_inverse(normal, inverse, 0.25, 3)
+    verified_inverse(normal, inverse, 0.25, 4)
     x = inverse[...]
     w = weights[...]
     out[...] = base[...] + fast(fast(h[...], x), h[...], ((1,), (1,)))

time: 69.4 us -> 82.3 us (1.19); the launches traced: 69.3 us -> 80.9 us
  Pallas kernels: 67.4 us -> 78.6 us
    pallas_call x1, Pallas kernels: 6.81 us -> 18.6 us  [body(): pl.pallas_call(first_kernel, out_shape=sds(NI, NI), in_specs=[v], out_spe...]
where the time goes in v7:
time: 82.3 us; the launch traced here: 80.9 us
  Pallas kernels  78.6 us (96%)
  local copies, waits for them, and re-layouts  1.16 us (1%)
  between operations  1.09 us (1%)
    pallas_call x1, Pallas kernels, body(): pl.pallas_call(second_kernel, out_shape=(sds(NS, NS), sds(NE, NS), sds(NI...  51.8 us
    pallas_call x1, Pallas kernels, body(): pl.pallas_call(first_kernel, out_shape=sds(NI, NI), in_specs=[v], out_spe...  18.6 us
    pallas_call x1, Pallas kernels, body(): pl.pallas_call(third_kernel, out_shape=(sds(NI, NI), sds(count, NRC)), in...  8.18 us

profile of v7, /device:TPU:1, one launch (start us, length us, event | category | flops | bytes accessed | tf_op | source)
XLA Modules:
  0.0 80.9 jit_solution(2095229283578076150)
XLA Ops:
  0.6 0.0 copy-start
  0.6 0.0 copy-start.1
  0.7 1.1 %copy-done.1 = f32[1,1,384,384]{3,2,1,0:T(8,128)S(1)} copy-done((f32[1,1,384,384]{3,2,1,0:T(8,128)S(1)}, f32[1,1,384,384]{3,2,1,0:T(8,128)}, u32[]{:S(2)}) %copy-start.1) | copy-done | bytes 589848
  1.8 0.0 copy-start.2
  1.8 0.0 copy-start.3
  1.8 0.0 copy-start.4
  1.8 0.0 copy-start.5
  1.8 18.6 %shard_map.77.ainv = f32[384,384]{1,0:T(8,128)S(1)} custom-call(f32[384,384]{1,0:T(8,128)S(1)} %bitcast.7), custom_call_target="tpu_custom_call" | custom-call | tf_op jit(solution)/shard_map/pallas_call | solution.py:381
  20.4 0.0 copy-done
  20.5 0.0 copy-done.2
  20.5 0.0 copy-done.3
  20.5 0.0 copy-done.4
  20.5 0.0 copy-done.5
  20.5 51.8 %shard_map.78 = (f32[384,384]{1,0:T(8,128)S(1)}, f32[256,384]{1,0:T(8,128)S(1)}, f32[384,384]{1,0:T(8,128)S(1)}, f32[384,384]{1,0:T(8,128)S(1)}, f32[40,384]{1,0:T(8,128)S(1)}, /*index=5*/f32[40,256]{1,0:T(8,128)S(1)}) custom-call(s32[1,5]{1,0:T(1,128)S(1)} %bitcast.9, f32[384,384]{1,0:T(8,128)S(1)} %shard_map.77.ainv, f32[384,640]{1,0:T(8,128)S(1)} %bitcast.6, ...), custom_call_target="tpu_custom_call" | custom-call | tf_op jit(solution)/shard_map/pallas_call | solution.py:388
  72.3 8.2 %shard_map.79 = (f32[384,384]{1,0:T(8,128)}, f32[40,640]{1,0:T(8,128)}) custom-call(f32[384,384]{1,0:T(8,128)S(1)} %get-tuple-element.10.normal, s32[1,384]{1,0:T(1,128)S(1)} %copy-done.3, f32[384,384]{1,0:T(8,128)S(1)} %get-tuple-element.11.base, f32[384,384]{1,0:T(8,128)S(1)} %get-tuple-element.12.h, f32[256,384]{1,0:T(8,128)S(1)} %get-tuple-element.13.weights, ...), custom_call_target="tpu_custom_call" | custom-call | tf_op jit(solution)/shard_map/pallas_call | solution.py:403
Async XLA Ops:
  0.6 19.8 %copy-start = (f32[1,1,384,640]{3,2,1,0:T(8,128)S(1)}, f32[1,1,384,640]{3,2,1,0:T(8,128)}, u32[]{:S(2)}) copy-start(f32[1,1,384,640]{3,2,1,0:T(8,128)} %param.7) | copy-start | bytes 2949124
  0.6 1.1 %copy-start.1 = (f32[1,1,384,384]{3,2,1,0:T(8,128)S(1)}, f32[1,1,384,384]{3,2,1,0:T(8,128)}, u32[]{:S(2)}) copy-start(f32[1,1,384,384]{3,2,1,0:T(8,128)} %param.6) | copy-start | bytes 1769476
  1.8 18.7 %copy-start.2 = (f32[1,40,640]{2,1,0:T(8,128)S(1)}, f32[1,40,640]{2,1,0:T(8,128)}, u32[]{:S(2)}) copy-start(f32[1,40,640]{2,1,0:T(8,128)} %param.9) | copy-start | bytes 307204
  1.8 18.7 %copy-start.3 = (s32[1,384]{1,0:T(1,128)S(1)}, s32[1,384]{1,0:T(1,128)}, u32[]{:S(2)}) copy-start(s32[1,384]{1,0:T(1,128)} %sep.3) | copy-start | bytes 4612
  1.8 18.7 %copy-start.4 = (f32[384]{0:T(512)S(1)}, f32[384]{0:T(512)}, u32[]{:S(2)}) copy-start(f32[384]{0:T(512)} %diag.1) | copy-start | bytes 4612
  1.8 18.7 %copy-start.5 = (s32[1,1,5]{2,1,0:T(1,128)S(1)}, s32[1,1,5]{2,1,0:T(1,128)}, u32[]{:S(2)}) copy-start(s32[1,1,5]{2,1,0:T(1,128)} %param.8) | copy-start | bytes 64
